TPU v7x, 32 devices: a whole 2x2x4 slice. The times are simulated.
32 devices in a mesh: dp: 8 (over z, x), tensor: 4 (over y, core).
Axes of the slice: x: 2, y: 2, z: 4, core: 2. Of those that a mesh axis runs over, the one named last changes fastest.
Arguments:
- tokens: bfloat16 [32768, 768], P(('dp', 'tensor')), may hold values from -6 to 6
- segment_ids: int32 [16, 2048], P('dp'), may hold values from 0 to 8, as said below
- memory_positions: int32 [16, 20], P('dp'), may hold values from 0 to 2047, as said below
- memory_rows: bfloat16 [20, 768], replicated, may hold values from -6 to 6
- qkv_weight: bfloat16 [768, 12, 192], P('dp', 'tensor'), may hold values from -0.21875 to 0.21875
- qv_bias: bfloat16 [12, 128], P('tensor'), may hold values from -3 to 3
- out_weight: bfloat16 [768, 12, 64], P('dp', 'tensor'), may hold values from -0.875 to 0.875
- out_bias: bfloat16 [768], replicated, may hold values from -1.75 to 1.75
- norm1_gain: bfloat16 [768], replicated, may hold values from 0.5 to 1.5
- norm1_bias: bfloat16 [768], replicated, may hold values from -1.75 to 1.75
- up_weight: bfloat16 [768, 3072], P('dp', 'tensor'), may hold values from -0.21875 to 0.21875
- up_bias: bfloat16 [3072], P('tensor'), may hold values from -3 to 3
- down_weight: bfloat16 [768, 3072], P('dp', 'tensor'), may hold values from -0.109375 to 0.109375
- down_bias: bfloat16 [768], replicated, may hold values from -1.75 to 1.75
- norm2_gain: bfloat16 [768], replicated, may hold values from 0.5 to 1.5
- norm2_bias: bfloat16 [768], replicated, may hold values from -1.75 to 1.75
- out_cotangent: bfloat16 [32768, 768], P(('dp', 'tensor')), may hold values from -6 to 6
Outputs:
- block_out: bfloat16 [32768, 768], P(('dp', 'tensor'))
- grad_tokens: float32 [32768, 768], P(('dp', 'tensor'))
- grad_memory_rows: float32 [20, 768], replicated
- grad_qkv_weight: float32 [768, 12, 192], P('dp', 'tensor')
- grad_qv_bias: float32 [12, 128], P('tensor')
- grad_out_weight: float32 [768, 12, 64], P('dp', 'tensor')
- grad_out_bias: float32 [768], replicated
- grad_norm1_gain: float32 [768], replicated
- grad_norm1_bias: float32 [768], replicated
- grad_up_weight: float32 [768, 3072], P('dp', 'tensor')
- grad_up_bias: float32 [3072], P('tensor')
- grad_down_weight: float32 [768, 3072], P('dp', 'tensor')
- grad_down_bias: float32 [768], replicated
- grad_norm2_gain: float32 [768], replicated
- grad_norm2_bias: float32 [768], replicated
Inputs may be any that keep to these rules, and one draw needn't show every extreme that they name: `segment_ids`: never falling along a group; each group begins with segment 0 of at least 512 positions and holds every segment up to 8. `memory_positions`: within a group all positions differ; read rows lie among the first 512 positions, the first at 0, write rows among the last 512, the first at 2047.
All inputs are finite; a program needn't handle non-finite values.
Results may differ from a plain program's by a relative error of at most 0.015.
Values may be sent and summed in bfloat16 or wider, within the bound.
A program may use at most 192 MiB of HBM per device.

v0:
```python
import functools

import jax
import jax.numpy as jnp
from jax import lax
from jax.experimental import pallas as pl
from jax.experimental.pallas import tpu as pltpu
from jax.sharding import PartitionSpec as P

EPSILON = 1e-12
TILE = 256
MASKED = -1e30
VMEM_MAX = 64 * 1024 * 1024 - 128 * 1024
NT = (((1,), (1,)), ((), ()))
NN = (((1,), (0,)), ((), ()))


def mm(a, b, dims=NN):
    return lax.dot_general(a, b, dims, preferred_element_type=jnp.float32)


def fold8(x):
    r = x.shape[0]
    return x.reshape(r // 8, 8, x.shape[1])


def head_masks(block):
    lane = lax.broadcasted_iota(jnp.int32, block.shape, 1)
    zero = jnp.zeros_like(block)
    return jnp.where(lane < 64, block, zero), jnp.where(lane < 64, zero, block)


def tile_visible(first_ref, last_ref, i, t):
    return (first_ref[t] == 0) | ((first_ref[t] <= last_ref[i]) & (last_ref[t] >= first_ref[i]))


def forward_kernel(first_ref, last_ref, q_ref, k_ref, v_ref, kseg_ref, qseg_ref, o_ref, lse_ref,
                   vt_ref, qm_ref, s_ref, m_ref, l_ref, acc_ref):
    i = pl.program_id(0)
    tiles = pl.num_programs(0)
    pairs = q_ref.shape[1] // 128
    heads = 2 * pairs

    @pl.when(i == 0)
    def _():
        def turn(t, c):
            rows = pl.ds(pl.multiple_of(t * TILE, TILE), TILE)
            vt_ref[t] = v_ref[rows, :].T
            return c
        lax.fori_loop(0, tiles, turn, 0)

    for g in range(pairs):
        a, b = head_masks(q_ref[:, 128 * g:128 * g + 128])
        qm_ref[2 * g] = a
        qm_ref[2 * g + 1] = b
    m_ref[...] = jnp.full_like(m_ref, MASKED)
    l_ref[...] = jnp.zeros_like(l_ref)
    acc_ref[...] = jnp.zeros_like(acc_ref)
    qseg = qseg_ref[0:1, :]

    def scores(t, c):
        @pl.when(tile_visible(first_ref, last_ref, i, t))
        def _():
            rows = pl.ds(pl.multiple_of(t * TILE, TILE), TILE)
            kseg = kseg_ref[rows, :]
            kseg = jnp.concatenate([kseg, kseg], axis=1)
            seen = (kseg == 0) | (kseg == qseg)
            for h in range(heads):
                kp = k_ref[rows, 128 * (h // 2):128 * (h // 2) + 128]
                s = mm(kp, qm_ref[h], NT)
                s = jnp.where(seen, s, MASKED)
                s_ref[h, t] = s
                m_ref[h] = jnp.maximum(m_ref[h], jnp.max(fold8(s), axis=0))
        return c
    lax.fori_loop(0, tiles, scores, 0)
    for h in range(heads):
        m_ref[h] = jnp.broadcast_to(jnp.max(m_ref[h], axis=0, keepdims=True), (8, TILE))

    def mix(t, c):
        @pl.when(tile_visible(first_ref, last_ref, i, t))
        def _():
            for h in range(heads):
                p = jnp.exp(s_ref[h, t] - m_ref[h, 0:1, :])
                l_ref[h] = l_ref[h] + jnp.sum(fold8(p), axis=0)
                acc_ref[h] = acc_ref[h] + mm(vt_ref[t, 64 * h:64 * h + 64, :], p.astype(jnp.bfloat16))
        return c
    lax.fori_loop(0, tiles, mix, 0)
    for h in range(heads):
        total = jnp.sum(l_ref[h], axis=0, keepdims=True)
        lse_ref[h:h + 1, :] = m_ref[h, 0:1, :] + jnp.log(total)
        acc_ref[h] = acc_ref[h] / total
    for g in range(pairs):
        pair = jnp.concatenate([acc_ref[2 * g], acc_ref[2 * g + 1]], axis=0)
        o_ref[:, 128 * g:128 * g + 128] = pair.T.astype(jnp.bfloat16)


def attend_forward(q, k, v, seg):
    n, width = q.shape
    tiles = n // TILE
    heads = width // 64
    first = seg[::TILE]
    last = seg[TILE - 1::TILE]
    kseg = jnp.broadcast_to(seg[:, None], (n, 128))
    qseg = jnp.broadcast_to(seg[None, :], (8, n))
    whole = lambda shape: pl.BlockSpec(shape, lambda i, *_: (0,) * len(shape))
    return pl.pallas_call(
        forward_kernel,
        out_shape=(jax.ShapeDtypeStruct((n, width), jnp.bfloat16), jax.ShapeDtypeStruct((8, n), jnp.float32)),
        grid_spec=pltpu.PrefetchScalarGridSpec(
            num_scalar_prefetch=2, grid=(tiles,),
            in_specs=[pl.BlockSpec((TILE, width), lambda i, *_: (i, 0)), whole((n, width)), whole((n, width)),
                      whole((n, 128)), pl.BlockSpec((8, TILE), lambda i, *_: (0, i))],
            out_specs=[pl.BlockSpec((TILE, width), lambda i, *_: (i, 0)), pl.BlockSpec((8, TILE), lambda i, *_: (0, i))],
            scratch_shapes=[
                pltpu.VMEM((tiles, width, TILE), jnp.bfloat16),
                pltpu.VMEM((heads, TILE, 128), jnp.bfloat16),
                pltpu.VMEM((heads, tiles, TILE, TILE), jnp.float32),
                pltpu.VMEM((heads, 8, TILE), jnp.float32),
                pltpu.VMEM((heads, 8, TILE), jnp.float32),
                pltpu.VMEM((heads, 64, TILE), jnp.float32),
            ]),
        compiler_params=pltpu.CompilerParams(dimension_semantics=("arbitrary",), vmem_limit_bytes=VMEM_MAX),
        cost_estimate=pl.CostEstimate(flops=4 * n * n * width, bytes_accessed=8 * n * width, transcendentals=n * n * heads),
        name="attend_forward",
    )(first, last, q, k, v, kseg, qseg)


def backward_kernel(base, first_ref, last_ref, q_ref, do_ref, o_ref, k_ref, v_ref, kseg_ref, qseg_ref, lse_ref,
                    d_ref, kt_ref, qm_ref, dom_ref, delta_ref, dqt_ref, dka_ref, dva_ref):
    i = pl.program_id(0)
    tiles = pl.num_programs(0)

    @pl.when(i == 0)
    def _():
        def turn(t, c):
            rows = pl.ds(pl.multiple_of(t * TILE, TILE), TILE)
            kt_ref[t] = k_ref[rows, :].T
            dka_ref[rows, :] = jnp.zeros((TILE, 128), jnp.float32)
            dva_ref[rows, :] = jnp.zeros((TILE, 128), jnp.float32)
            return c
        lax.fori_loop(0, tiles, turn, 0)

    for ref, masked in ((q_ref, qm_ref), (do_ref, dom_ref)):
        masked[0], masked[1] = head_masks(ref[...])
    inner = (do_ref[...].astype(jnp.float32) * o_ref[...].astype(jnp.float32)).T
    for h in range(2):
        delta_ref[h] = jnp.broadcast_to(jnp.sum(inner[64 * h:64 * h + 64], axis=0, keepdims=True), (8, TILE))
    dqt_ref[...] = jnp.zeros_like(dqt_ref)
    qseg = qseg_ref[0:1, :]

    def count(t, c):
        prompt, before, upto = c
        return (prompt + (first_ref[t] == 0).astype(jnp.int32), before + (last_ref[t] < first_ref[i]).astype(jnp.int32),
                upto + (first_ref[t] <= last_ref[i]).astype(jnp.int32))
    zero = jnp.int32(0)
    prompt, before, upto = lax.fori_loop(0, tiles, count, (zero, zero, zero))
    start = jnp.maximum(prompt, before)
    visible = prompt + jnp.maximum(upto - start, 0)

    def one_tile(n):
        t = jnp.where(n < prompt, n, start + n - prompt)
        rows = pl.ds(pl.multiple_of(t * TILE, TILE), TILE)
        kseg = kseg_ref[rows, :]
        kseg = jnp.concatenate([kseg, kseg], axis=1)
        seen = (kseg == 0) | (kseg == qseg)
        kp = k_ref[rows, :]
        vp = v_ref[rows, :]
        s = [mm(kp, qm_ref[h], NT) for h in range(2)]
        d = [mm(vp, dom_ref[h], NT) for h in range(2)]
        p = [jnp.where(seen, jnp.exp(s[h] - lse_ref[base + h:base + h + 1, :]), 0.0) for h in range(2)]
        ds = [(p[h] * (d[h] - delta_ref[h, 0:1, :])).astype(jnp.bfloat16) for h in range(2)]
        p = [value.astype(jnp.bfloat16) for value in p]
        dva_ref[rows, :] = dva_ref[rows, :] + (mm(p[0], dom_ref[0]) + mm(p[1], dom_ref[1]))
        dka_ref[rows, :] = dka_ref[rows, :] + (mm(ds[0], qm_ref[0]) + mm(ds[1], qm_ref[1]))
        return [mm(kt_ref[t, 64 * h:64 * h + 64, :], ds[h]) for h in range(2)]

    def two_tiles(n, c):
        one, two = one_tile(2 * n), one_tile(2 * n + 1)
        for h in range(2):
            dqt_ref[h] = dqt_ref[h] + (one[h] + two[h])
        return c
    lax.fori_loop(0, visible // 2, two_tiles, 0)

    @pl.when(visible % 2 == 1)
    def _():
        for h, value in enumerate(one_tile(visible - 1)):
            dqt_ref[h] = dqt_ref[h] + value
    pair = jnp.concatenate([dqt_ref[0], dqt_ref[1]], axis=0)
    own = pl.ds(pl.multiple_of(i * TILE, TILE), TILE)
    d_ref[own, 0:128] = (pair.T * 0.125).astype(jnp.bfloat16)

    @pl.when(i == tiles - 1)
    def _():
        d_ref[:, 128:256] = dka_ref[...].astype(jnp.bfloat16)
        d_ref[:, 256:384] = dva_ref[...].astype(jnp.bfloat16)


def attend_backward(g, q, k, v, do, o, lse, seg):
    n, width = q.shape[0], 128
    tiles = n // TILE
    heads = width // 64
    first = seg[::TILE]
    last = seg[TILE - 1::TILE]
    kseg = jnp.broadcast_to(seg[:, None], (n, 128))
    qseg = jnp.broadcast_to(seg[None, :], (8, n))
    whole = lambda shape: pl.BlockSpec(shape, lambda i, *_: (0,) * len(shape))
    rows = pl.BlockSpec((TILE, width), lambda i, *_: (i, g))
    column = pl.BlockSpec((n, width), lambda i, *_: (0, g))
    stat = pl.BlockSpec((8, TILE), lambda i, *_: (0, i))
    return pl.pallas_call(
        functools.partial(backward_kernel, 2 * g),
        out_shape=jax.ShapeDtypeStruct((n, 3 * width), jnp.bfloat16),
        grid_spec=pltpu.PrefetchScalarGridSpec(
            num_scalar_prefetch=2, grid=(tiles,),
            in_specs=[rows, rows, rows, column, column, whole((n, 128)), stat, stat],
            out_specs=whole((n, 3 * width)),
            scratch_shapes=[
                pltpu.VMEM((tiles, width, TILE), jnp.bfloat16),
                pltpu.VMEM((heads, TILE, 128), jnp.bfloat16),
                pltpu.VMEM((heads, TILE, 128), jnp.bfloat16),
                pltpu.VMEM((heads, 8, TILE), jnp.float32),
                pltpu.VMEM((heads, 64, TILE), jnp.float32),
                pltpu.VMEM((n, width), jnp.float32),
                pltpu.VMEM((n, width), jnp.float32),
            ]),
        compiler_params=pltpu.CompilerParams(dimension_semantics=("arbitrary",), vmem_limit_bytes=VMEM_MAX),
        cost_estimate=pl.CostEstimate(flops=10 * n * n * width, bytes_accessed=14 * n * width, transcendentals=n * n * heads),
        name="attend_backward",
    )(first, last, q, do, o, k, v, kseg, qseg, lse)


BLOCK = 256
STRIP = 64


def normal_cdf_parts(u):
    v = u * 0.7071067811865476
    c = jnp.clip(v, -3.832506856900711, 3.832506856900711)
    c2 = c * c
    top = 0.00022905065861350646
    for a in (0.0034082910107109506, 0.050955695062380861, 0.18520832239976145, 1.128379143519084):
        top = top * c2 + a
    low = -1.1791602954361697e-7
    for b in (0.000023547966471313185, 0.0010179625278914885, 0.014070470171167667, 0.11098505178285362,
              0.49746925110067538, 1.0):
        low = low * c2 + b
    cdf = 0.5 + 0.5 * (c * top / low)
    slope = jnp.exp(-(v * v)) * (u * 0.3989422804014327)
    return u * cdf, cdf + slope


def middle_kernel(pieces, o_all, x0, outs, ups, downs, cot, vec_ref, bup_ref,
                  block_out, dr1, do_all, g_down, g_up, g_out, sums_ref, upsum_ref,
                  o_ref, raw_ref, wo_ref, wu_ref, wd_ref, hat_ref, inv_ref, acc_ref, hl_ref, hlt_ref, gp_ref, z_ref, c_ref,
                  df_ref, dft_ref, y_ref, st_ref, su_ref, ru_ref, rd_ref, go_ref, rgo_ref, u0_ref, u1_ref,
                  sem, osem, send, recv):
    f32, bf16 = jnp.float32, jnp.bfloat16
    rows, width = hat_ref.shape
    blocks = rows // BLOCK
    part = wu_ref.shape[2]
    bf = lambda a: a.astype(bf16)
    dp, tensor = lax.axis_index("dp"), lax.axis_index("tensor")
    inner = tensor % 2
    partner = (dp, tensor + 1 - 2 * inner)
    z = dp // 2
    to_y = (dp, (tensor + 2) % 4)
    mine = pl.multiple_of(inner * rows, 1024)
    theirs = pl.multiple_of((1 - inner) * rows, 1024)
    greet([partner, to_y] if pieces else [partner])

    def remote(n, src, dst, device=partner):
        return pltpu.make_async_remote_copy(src, dst, send.at[n], recv.at[n], device_id=device,
                                            device_id_type=pl.DeviceIdType.MESH)

    swap_o = remote(0, o_all.at[pl.ds(theirs, rows), :], o_ref.at[1])
    swap_o.start()
    count = [0]

    def load(src, dst):
        copy = pltpu.make_async_copy(src, dst, sem.at[count[0]])
        count[0] += 1
        copy.start()
        return copy

    def weight(sources, dst):
        if not pieces:
            return [load(sources[0].at[o], dst.at[o]) for o in range(2)]
        digit = dp % 2
        made = []
        for o in range(2):
            for zi in range(sources[0].shape[1]):
                for n in range(2):
                    place = 2 * zi + (digit if n == 0 else 1 - digit)
                    r = sources[n].shape[2]
                    made.append(load(sources[n].at[o, zi], dst.at[o, pl.ds(pl.multiple_of(place * r, r), r), :]))
        return made

    if pieces:
        r = downs[0].shape[0]
        block = lambda o, zi: wd_ref.at[o, pl.ds(pl.multiple_of(zi * r, r), r), :]
        zs = [(z + 4 - k) % 4 for k in range(4)]
        held = [load(downs[k], block(0, zs[k])) for k in range(4)]
    first = [load(o_all.at[pl.ds(mine, rows), :], o_ref.at[0]), load(x0, hat_ref)] + weight(outs, raw_ref.at[0])
    if pieces:
        second = [load(ups[o], wu_ref.at[o]) for o in range(2)]
    else:
        second = [load(ups[0].at[o], wu_ref.at[o]) for o in range(2)]
    if not pieces:
        second = second + weight(downs, wd_ref)
    late = load(cot, c_ref)
    if pieces:
        by_y = []
        for k in range(4):
            held[k].wait()
            by_y.append(remote(12 + k, block(0, zs[k]), block(1, zs[k]), to_y))
            by_y[k].start()
    vec = lambda n: vec_ref[n:n + 1, :]
    sums_ref[...] = jnp.zeros_like(sums_ref)
    upsum_ref[...] = jnp.zeros_like(upsum_ref)
    for copy in first:
        copy.wait()
    swaps = [remote(1, raw_ref.at[0], raw_ref.at[1])]
    swaps[0].start()
    for copy in second:
        copy.wait()
    for o in range(2):
        swaps.append(remote(2 + 2 * o, wu_ref.at[o], wu_ref.at[2 + o]))
        swaps.append(remote(3 + 2 * o, wd_ref.at[o], wd_ref.at[2 + o]))
    for copy in swaps[1:4] if pieces else swaps[1:]:
        copy.start()
    lane = lax.broadcasted_iota(jnp.int32, (width, 128), 1)

    def order_heads(side):
        wo_ref[side, :, 0:128] = raw_ref[side, 0, :, 0:128]
        wo_ref[side, :, 128:256] = raw_ref[side, 1, :, 0:128]
        upper = pltpu.roll(raw_ref[side, 1, :, 128:256].astype(f32), 64, 1)
        wo_ref[side, :, 256:384] = bf(jnp.where(lane < 64, raw_ref[side, 0, :, 128:256].astype(f32), upper))
    order_heads(0)
    swaps[0].wait()
    order_heads(1)
    swap_o.wait()

    def strips(body):
        def run(s, carry):
            body(pl.ds(pl.multiple_of(s * STRIP, STRIP), STRIP))
            return carry
        lax.fori_loop(0, rows // STRIP, run, 0)

    def add_sum(n, value):
        sums_ref[n] = sums_ref[n] + jnp.sum(fold(value), axis=0)

    def fold(value):
        return value.reshape(value.shape[0] // 8, 8, value.shape[1])

    def mean(value):
        return jnp.sum(value, axis=-1, keepdims=True) * (1.0 / width)

    def project(b, carry):
        r = pl.ds(pl.multiple_of(b * BLOCK, BLOCK), BLOCK)
        acc_ref[r, :] = mm(o_ref[0, r, :], wo_ref[0], NT) + mm(o_ref[1, r, :], wo_ref[1], NT)
        return carry
    lax.fori_loop(0, blocks, project, 0)

    def first_norm(r):
        r1 = hat_ref[r, :] + (acc_ref[r, :] + vec(0))
        centre = r1 - mean(r1)
        inv = lax.rsqrt(mean(centre * centre) + EPSILON)
        hat = centre * inv
        hat_ref[r, :] = hat
        inv_ref[r, :] = inv
        hl_ref[r, :] = bf(hat * vec(1) + vec(2))
    strips(first_norm)
    for b in range(blocks):
        hlt_ref[:, BLOCK * b:BLOCK * b + BLOCK] = hl_ref[BLOCK * b:BLOCK * b + BLOCK, :].T
    acc_ref[...] = jnp.zeros_like(acc_ref)

    bufs = (u0_ref, u1_ref)

    def forward(n, carry):
        j = n % 2 * 2 + n // 2
        for o in range(2):
            @pl.when(j == 2 + o)
            def _(o=o):
                swaps[1 + 2 * o].wait()
                swaps[2 + 2 * o].wait()
        if pieces:
            @pl.when(j == 1)
            def _():
                for copy in by_y:
                    copy.wait()
                swaps[4].start()

        def lift(b):
            bufs[b % 2][...] = mm(hl_ref[BLOCK * b:BLOCK * b + BLOCK, :], wu_ref[j]) + bup_ref[j, 0:1, :].astype(f32)
        lift(0)
        for b in range(blocks):
            if b + 1 < blocks:
                lift(b + 1)
            r = slice(BLOCK * b, BLOCK * b + BLOCK)
            for i in range(0, BLOCK, 32):
                for w in range(0, part, 256):
                    z, gp = normal_cdf_parts(bufs[b % 2][i:i + 32, w:w + 256])
                    z_ref[j, BLOCK * b + i:BLOCK * b + i + 32, w:w + 256] = bf(z)
                    gp_ref[j, BLOCK * b + i:BLOCK * b + i + 32, w:w + 256] = gp
            acc_ref[r, :] = acc_ref[r, :] + mm(z_ref[j, r, :], wd_ref[j], NT)
        return carry
    lax.fori_loop(0, 4, forward, 0)
    late.wait()

    def second_norm(r):
        h1 = hat_ref[r, :] * vec(1) + vec(2)
        r2 = h1 + (acc_ref[r, :] + vec(3))
        centre = r2 - mean(r2)
        inv = lax.rsqrt(mean(centre * centre) + EPSILON)
        hat = centre * inv
        y_ref[r, :] = bf(hat * vec(4) + vec(5))
        c = c_ref[r, :].astype(f32)
        add_sum(0, c * hat)
        add_sum(1, c)
        w = c * vec(4)
        dr2 = (w - mean(w) - hat * mean(w * hat)) * inv
        acc_ref[r, :] = dr2
        low = bf(dr2)
        df_ref[r, :] = low
        add_sum(2, low.astype(f32))
    strips(second_norm)
    stores = [pltpu.make_async_copy(y_ref, block_out, osem.at[0])]
    stores[0].start()
    for b in range(blocks):
        dft_ref[:, BLOCK * b:BLOCK * b + BLOCK] = df_ref[BLOCK * b:BLOCK * b + BLOCK, :].T

    def backward(n, carry):
        j = 3 - n

        def lower(b):
            bufs[b % 2][...] = mm(df_ref[BLOCK * b:BLOCK * b + BLOCK, :], wd_ref[j])
        slot = n % 2
        away = [remote(6 + slot, st_ref.at[slot], rd_ref.at[slot]), remote(8 + slot, su_ref.at[slot], ru_ref.at[slot])]
        lower(0)
        for b in range(blocks):
            if b + 1 < blocks:
                lower(b + 1)
            r = slice(BLOCK * b, BLOCK * b + BLOCK)
            for i in range(0, BLOCK, 64):
                q = slice(BLOCK * b + i, BLOCK * b + i + 64)
                dul = bf(bufs[b % 2][i:i + 64, :] * gp_ref[j, q, :])
                upsum_ref[j] = upsum_ref[j] + jnp.sum(fold(dul.astype(f32)), axis=0)
                hat2_ref[q, :] = dul
            acc_ref[r, :] = acc_ref[r, :] + mm(hat2_ref[r, :], wu_ref[j], NT)

        @pl.when(n < 2)
        def _():
            for m in range(0, width, BLOCK):
                st_ref[slot, m:m + BLOCK, :] = bf(mm(dft_ref[m:m + BLOCK, :], z_ref[j]))
            away[0].start()
            for m in range(0, width, BLOCK):
                su_ref[slot, m:m + BLOCK, :] = bf(mm(hlt_ref[m:m + BLOCK, :], hat2_ref[...]))
            away[1].start()

        @pl.when(n >= 2)
        def _():
            away[0].wait()
            for m in range(0, width, BLOCK):
                got = rd_ref[slot, m:m + BLOCK, :].astype(f32)
                st_ref[slot, m:m + BLOCK, :] = bf(mm(dft_ref[m:m + BLOCK, :], z_ref[j]) + got)
            if pieces:
                @pl.when(j == 0)
                def _():
                    pltpu.make_async_copy(st_ref.at[1], g_down[0], osem.at[2]).start()

                @pl.when(j == 1)
                def _():
                    early.start()
                    pltpu.make_async_copy(st_ref.at[0, width // 2:, :], g_down[1], osem.at[1]).start()
            else:
                pltpu.make_async_copy(st_ref.at[slot], g_down.at[j], osem.at[1 + slot]).start()
            away[1].wait()
            for m in range(0, width, BLOCK):
                got = ru_ref[slot, m:m + BLOCK, :].astype(f32)
                su_ref[slot, m:m + BLOCK, :] = bf(mm(hlt_ref[m:m + BLOCK, :], hat2_ref[...]) + got)
            if pieces:
                r = g_up[0].shape[2]
                for zi in range(g_up[0].shape[1]):
                    for o in range(2):
                        at = pl.multiple_of((2 * zi + (dp + o) % 2) * r, r)
                        pltpu.make_async_copy(su_ref.at[slot, pl.ds(at, r), :], g_up[o].at[j, zi], osem.at[3 + slot]).start()
            else:
                pltpu.make_async_copy(su_ref.at[slot], g_up.at[j], osem.at[3 + slot]).start()
        return carry
    hat2_ref = y_ref
    stores[0].wait()
    if pieces:
        early = remote(16, st_ref.at[0, 0:width // 2, :], g_down[2], to_y)
    lax.fori_loop(0, 4, backward, 0)

    def first_back(r):
        dh1 = acc_ref[r, :]
        hat = hat_ref[r, :]
        add_sum(3, dh1 * hat)
        add_sum(4, dh1)
        w = dh1 * vec(1)
        grad = (w - mean(w) - hat * mean(w * hat)) * inv_ref[r, :]
        acc_ref[r, :] = grad
        low = bf(grad)
        df_ref[r, :] = low
        add_sum(5, low.astype(f32))
    strips(first_back)
    out = pltpu.make_async_copy(acc_ref, dr1, osem.at[0])
    out.start()
    stores = [out]
    for b in range(blocks):
        dft_ref[:, BLOCK * b:BLOCK * b + BLOCK] = df_ref[BLOCK * b:BLOCK * b + BLOCK, :].T
    lane = lax.broadcasted_iota(jnp.int32, (BLOCK, 128), 1)

    def out_grad(side, m):
        tiles = [mm(dft_ref[m:m + BLOCK, :], o_ref[side, :, 128 * g:128 * g + 128]) for g in range(3)]
        third = [jnp.where(lane < 64, tiles[2], 0.0), jnp.where(lane < 64, pltpu.roll(tiles[2], 64, 1), 0.0)]
        return [jnp.concatenate([tiles[o], third[o]], axis=1) for o in range(2)]
    for m in range(0, width, BLOCK):
        for o, value in enumerate(out_grad(1, m)):
            go_ref[o, m:m + BLOCK, :] = bf(value)
    swap_go = remote(10, go_ref, rgo_ref)
    swap_go.start()
    ow = wo_ref.shape[2]
    for side in (1, 0):
        def push(b, carry):
            r = pl.ds(pl.multiple_of(b * BLOCK, BLOCK), BLOCK)
            y_ref[r, ow * side:ow * side + ow] = bf(mm(df_ref[r, :], wo_ref[side]))
            return carry
        lax.fori_loop(0, blocks, push, 0)
        if side == 1:
            swap_do = remote(11, y_ref.at[:, pl.ds(ow, ow)], do_all.at[pl.ds(mine, rows), :])
            swap_do.start()
        else:
            copy = pltpu.make_async_copy(y_ref.at[:, pl.ds(0, ow)], do_all.at[pl.ds(mine, rows), :], osem.at[5])
            copy.start()
            stores.append(copy)
    swap_go.wait()
    for m in range(0, width, BLOCK):
        for o, value in enumerate(out_grad(0, m)):
            go_ref[o, m:m + BLOCK, :] = bf(value + rgo_ref[o, m:m + BLOCK, :].astype(f32))
    for o in range(2 if pieces else 1):
        copy = pltpu.make_async_copy(go_ref.at[o] if pieces else go_ref, g_out[o] if pieces else g_out, osem.at[6 + o])
        copy.start()
        stores.append(copy)
    whole = g_down[0] if pieces else g_down.at[0]
    for slot in range(2):
        if pieces and slot == 0:
            pltpu.make_async_copy(st_ref.at[0, width // 2:, :], g_down[1], osem.at[1]).wait()
        else:
            pltpu.make_async_copy(st_ref.at[slot], whole, osem.at[1 + slot]).wait()
        pltpu.make_async_copy(su_ref.at[slot], whole, osem.at[3 + slot]).wait()
    if pieces:
        early.wait()
    swap_do.wait()
    for copy in stores:
        copy.wait()


def middle(o_all, x0, outs, ups, downs, cot, vec, bup):
    f32, bf16 = jnp.float32, jnp.bfloat16
    rows, width = x0.shape
    ow = o_all.shape[1]
    part = bup.shape[-1]
    pieces = len(ups) == 2
    shape = jax.ShapeDtypeStruct
    hbm = pl.BlockSpec(memory_space=pl.ANY)
    vmem = pl.BlockSpec(memory_space=pltpu.VMEM)
    v = pltpu.VMEM
    n = len(ups)
    m = 2 * n + len(downs)

    def kernel(o_all, x0, *refs):
        weights, rest = refs[:m], refs[m:]
        if pieces:
            rest = rest[:6] + (rest[6:9], rest[9:11], rest[11:13]) + rest[13:]
        middle_kernel(pieces, o_all, x0, weights[:n], weights[n:2 * n], weights[2 * n:], *rest)

    if pieces:
        parts = (2, len(downs), downs[0].shape[0] // 2, part)
        grads = [shape((width, part), bf16)] + [shape((width // 2, part), bf16)] * 2 + [shape(parts, bf16)] * 2 + [shape((width, 256), bf16)] * 2
    else:
        grads = [shape((2, width, part), bf16), shape((2, width, part), bf16), shape((2, width, 256), bf16)]
    return pl.pallas_call(
        kernel,
        out_shape=(shape((rows, width), bf16), shape((rows, width), f32), shape((2 * rows, ow), bf16),
                   *grads, shape((6, 8, width), f32), shape((4, 8, part), f32)),
        in_specs=[hbm] * (3 + m) + [vmem] * 2,
        out_specs=[hbm] * (3 + len(grads)) + [vmem] * 2,
        scratch_shapes=[
            v((2, rows, ow), bf16), v((2, 2, width, 256), bf16), v((2, width, ow), bf16), v((4, width, part), bf16),
            v((4, width, part), bf16),
            v((rows, width), f32), v((rows, 1), f32), v((rows, width), f32), v((rows, width), bf16), v((width, rows), bf16),
            v((4, rows, part), f32), v((4, rows, part), bf16), v((rows, width), bf16), v((rows, width), bf16),
            v((width, rows), bf16), v((rows, width), bf16), v((2, width, part), bf16),
            v((2, width, part), bf16), v((2, width, part), bf16), v((2, width, part), bf16), v((2, width, 256), bf16),
            v((2, width, 256), bf16), v((BLOCK, part), f32), v((BLOCK, part), f32),
            pltpu.SemaphoreType.DMA((40,)), pltpu.SemaphoreType.DMA((8,)),
            pltpu.SemaphoreType.DMA((24,)), pltpu.SemaphoreType.DMA((24,)),
        ],
        compiler_params=pltpu.CompilerParams(vmem_limit_bytes=VMEM_MAX, collective_id=1, has_side_effects=True),
        cost_estimate=pl.CostEstimate(flops=6 * rows * width * 9 * width, bytes_accessed=60_000_000, transcendentals=2 * rows * 4 * part),
        name="middle",
    )(o_all, x0, *outs, *ups, *downs, cot, vec, bup)


class Exchange:
    def __init__(self, send, recv):
        self.send, self.recv, self.used = send, recv, 0

    def copy(self, src, dst, device):
        n = self.used
        self.used += 1
        return pltpu.make_async_remote_copy(src, dst, self.send.at[n], self.recv.at[n], device_id=device,
                                            device_id_type=pl.DeviceIdType.MESH)


def greet(devices):
    barrier = pltpu.get_barrier_semaphore()
    for device in devices:
        pl.semaphore_signal(barrier, inc=1, device_id=device, device_id_type=pl.DeviceIdType.MESH)
    pl.semaphore_wait(barrier, len(devices))


def entry_kernel(tokens, pos_ref, mem_ref, wq_ref, bq_ref, bu_ref, wu_ref, wd_ref, wo_ref,
                 x0_out, x_out, q_out, k_out, v_out, w_out, up_g, down_g, out_g, bu_out,
                 x0_ref, x_ref, g_ref, b_ref, y_ref, third_ref, q_ref, k_ref, v_ref, ub_ref, send, recv, sem):
    f32, bf16 = jnp.float32, jnp.bfloat16
    rows, width = x0_ref.shape
    dp, tensor = lax.axis_index("dp"), lax.axis_index("tensor")
    z, x = dp // 2, dp % 2
    inner = tensor % 2
    zs = [(z + 4 - k) % 4 for k in range(4)]
    at = [2 * zs[k] + x for k in range(4)]
    far = [2 * zs[k] + 1 - x for k in range(4)]
    to_z = [None] + [(2 * ((z + k) % 4) + x, tensor) for k in range(1, 4)]
    to_x = (2 * z + 1 - x, tensor)
    to_y = (dp, (tensor + 2) % 4)
    to_core = (dp, tensor + 1 - 2 * inner)
    to_both = (dp, 3 - tensor)
    greet(to_z[1:] + [to_x, to_y, to_core, to_both])
    ex = Exchange(send, recv)
    started = []

    def go(src, dst, device):
        copy = ex.copy(src, dst, device)
        copy.start()
        started.append(copy)
        return copy

    local = []

    def keep(src, dst):
        copy = pltpu.make_async_copy(src, dst, sem.at[len(local)])
        copy.start()
        local.append(copy)
        return copy

    own = keep(wq_ref, g_ref.at[0, at[0]])
    own_bias = keep(bq_ref, b_ref.at[0])
    z_q = [None] + [go(wq_ref, g_ref.at[0, at[0]], to_z[k]) for k in range(1, 4)]
    x_q = [go(wq_ref, g_ref.at[0, at[0]], to_x)]
    y_q = [go(wq_ref, g_ref.at[1, at[0]], to_y)]
    bias = go(bq_ref, b_ref.at[1], to_y)
    up_bias = [go(bu_ref, ub_ref.at[n - 1], to) for n, to in ((1, to_y), (2, to_core), (3, to_both))]

    mine = pl.multiple_of(inner * rows, 1024)
    positions = pos_ref[0:1, :]
    strip = 128

    def start(s, carry):
        r = pl.multiple_of(s * strip, strip)
        place = lax.broadcasted_iota(jnp.int32, (strip, positions.shape[1]), 0) + (inner * rows + r)
        picks = jnp.where(place == positions, 1.0, 0.0).astype(bf16)
        value = tokens[pl.ds(r, strip), :].astype(f32) + mm(picks, mem_ref[...])
        x0_ref[pl.ds(r, strip), :] = value
        x_ref[pl.ds(mine + r, strip), :] = value.astype(bf16)
        return carry
    lax.fori_loop(0, rows // strip, start, 0)
    keep(x0_ref, x0_out)
    core = go(x_ref.at[pl.ds(mine, rows), :], x_ref.at[pl.ds(mine, rows), :], to_core)

    for k in range(1, 4):
        z_q[k].wait_recv()
        x_q.append(go(g_ref.at[0, at[k]], g_ref.at[0, at[k]], to_x))
        y_q.append(go(g_ref.at[0, at[k]], g_ref.at[1, at[k]], to_y))
    z_u = [None] + [go(wu_ref, up_g.at[at[0]], to_z[k]) for k in range(1, 4)]
    z_o = [None] + [go(wo_ref, out_g.at[0, z], to_z[k]) for k in range(1, 4)]
    keep(wu_ref, up_g.at[at[0]])
    keep(wd_ref, down_g.at[x])
    keep(wo_ref, out_g.at[0, z])
    last = []
    for k in range(2):
        x_q[k].wait_recv()
        last.append(go(g_ref.at[0, far[k]], g_ref.at[1, far[k]], to_y))
    for k in range(2, 4):
        y_q[k].wait_recv()
        last.append(go(g_ref.at[1, at[k]], g_ref.at[1, at[k]], to_x))
    rest = [go(wd_ref, down_g.at[x], to_x), go(wu_ref, up_g.at[at[0]], to_x), go(wo_ref, out_g.at[1, z], to_y)]
    own.wait()
    own_bias.wait()
    for copy in x_q[2:] + [core]:
        copy.wait_recv()
    keep(x_ref, x_out)
    lane = lax.broadcasted_iota(jnp.int32, (BLOCK, 128), 1)
    blocks = 2 * rows // BLOCK
    heads = (q_ref, k_ref, v_ref)

    def write(n, g, r, value):
        value = value.astype(bf16)
        if n == 0:
            value = value * jnp.asarray(0.125, bf16)
        heads[n][r, 128 * g:128 * g + 128] = value

    def project(o, b):
        r = pl.ds(pl.multiple_of(b * BLOCK, BLOCK), BLOCK)
        y_ref[:, 0:576] = mm(x_ref[r, :], g_ref[o].reshape(width, 576)) + b_ref[o, 0:1, 0:576].astype(f32)
        for n in range(3):
            write(n, o, r, y_ref[:, 128 * n:128 * n + 128])
        return r

    def project_own(b, carry):
        r = project(0, b)
        third_ref[r, :] = y_ref[:, 384:640]
        return carry

    def project_other(b, carry):
        r = project(1, b)
        turn = lambda value: pltpu.roll(value, 64, 1)
        left, right = third_ref[r, 0:128], y_ref[:, 384:512]
        write(0, 2, r, jnp.where(lane < 64, left, turn(right)))
        write(1, 2, r, jnp.where(lane < 64, turn(left), right))
        write(2, 2, r, jnp.where(lane < 64, third_ref[r, 128:256], turn(y_ref[:, 512:640])))
        return carry
    y_ref[...] = jnp.zeros_like(y_ref)
    lax.fori_loop(0, blocks, project_own, 0)
    for copy in y_q[:2] + last + [bias]:
        copy.wait_recv()
    keep(g_ref, w_out)
    for k in range(1, 4):
        z_u[k].wait_recv()
        rest.append(go(up_g.at[at[k]], up_g.at[at[k]], to_x))
        lax.fori_loop(blocks * (k - 1) // 4, blocks * k // 4, project_other, 0)
    lax.fori_loop(blocks * 3 // 4, blocks, project_other, 0)
    for src, dst in ((q_ref, q_out), (k_ref, k_out), (v_ref, v_out)):
        keep(src, dst)
    for k in range(1, 4):
        z_o[k].wait_recv()
        rest.append(go(out_g.at[0, zs[k]], out_g.at[1, zs[k]], to_y))
    for copy in rest + up_bias:
        copy.wait_recv()
    bu_out[0] = bu_ref[...]
    for n in range(3):
        bu_out[n + 1] = ub_ref[n]
    for copy in started:
        copy.wait_send()
    for copy in local[2:]:
        copy.wait()


def entry(tokens, positions, memory_rows, shard_qkv, biases, up_bias, up, down, out):
    f32, bf16 = jnp.float32, jnp.bfloat16
    rows, width = tokens.shape
    r = up.shape[0]
    shape, v = jax.ShapeDtypeStruct, pltpu.VMEM
    hbm, vmem = pl.BlockSpec(memory_space=pl.ANY), pl.BlockSpec(memory_space=pltpu.VMEM)
    qkv = shape((2 * rows, 384), bf16)
    return pl.pallas_call(
        entry_kernel,
        out_shape=(shape((rows, width), f32), shape((2 * rows, width), bf16), qkv, qkv, qkv,
                   shape((2, 8, r, 576), bf16), shape((8, r, up.shape[1]), bf16), shape((2, r, down.shape[1]), bf16),
                   shape((2, 4, r, out.shape[1]), bf16), shape((4, 16, up.shape[1]), bf16)),
        in_specs=[vmem] * 9,
        out_specs=[hbm] * 9 + [vmem],
        scratch_shapes=[
            v((rows, width), f32), v((2 * rows, width), bf16), v((2, 8, r, 576), bf16), v((2, 16, 640), bf16),
            v((BLOCK, 640), f32), v((2 * rows, 256), f32), v((2 * rows, 384), bf16), v((2 * rows, 384), bf16), v((2 * rows, 384), bf16),
            v((3, 16, up.shape[1]), bf16),
            pltpu.SemaphoreType.DMA((48,)), pltpu.SemaphoreType.DMA((48,)), pltpu.SemaphoreType.DMA((16,)),
        ],
        compiler_params=pltpu.CompilerParams(vmem_limit_bytes=VMEM_MAX, collective_id=0, has_side_effects=True),
        cost_estimate=pl.CostEstimate(flops=4 * rows * width * 1152, bytes_accessed=20_000_000, transcendentals=0),
        name="entry",
    )(tokens, positions, memory_rows, shard_qkv, biases, up_bias, up, down, out)


def exit_kernel(x_all, d0, d1, d2, w_all, third, kept_ref, came_ref, dr1, pos_ref, sums_in, up_in,
                tok_out, first_out, second_out, small_out,
                x_ref, xt_ref, d_ref, w_ref, dr_ref, g_ref, own_ref, oth_ref, yb_ref, xs_ref, xb_ref, zt_ref, zs_ref, zb_ref,
                fs_ref, fb_ref, their_ref, got_ref, tok_ref, s_ref, t_ref, r_ref, first_ref, send, recv, sem):
    f32, bf16 = jnp.float32, jnp.bfloat16
    rows, width = dr_ref.shape
    dp, tensor = lax.axis_index("dp"), lax.axis_index("tensor")
    z, x = dp // 2, dp % 2
    inner, outer = tensor % 2, tensor // 2
    up_z = [None] + [(z + k) % 4 for k in range(1, 4)]
    to_z = [None] + [(2 * up_z[k] + x, tensor) for k in range(1, 4)]
    to_x = (2 * z + 1 - x, tensor)
    to_y = (dp, (tensor + 2) % 4)
    to_core = (dp, tensor + 1 - 2 * inner)
    near_z = (2 * (z + 1 - 2 * (z % 2)) + x, tensor)
    far_z = to_z[2]
    loads = []
    for src, dst in ((d2, d_ref.at[2]), (x_all, x_ref), (d0, d_ref.at[0]), (d1, d_ref.at[1]),
                     (w_all.at[0, :, pl.ds(0, 384)], w_ref.at[0]), (w_all.at[1, :, pl.ds(0, 384)], w_ref.at[1]),
                     (third, w_ref.at[2]), (dr1, dr_ref)):
        copy = pltpu.make_async_copy(src, dst, sem.at[len(loads)])
        copy.start()
        loads.append(copy)
    greet(to_z[1:] + [to_x, to_y, to_core])
    ex = Exchange(send, recv)
    started = []

    def go(src, dst, device):
        copy = ex.copy(src, dst, device)
        copy.start()
        started.append(copy)
        return copy

    for k in range(4):
        first_ref[k] = kept_ref[k] + came_ref[k].astype(f32)
    for k in range(1, 4):
        fs_ref[k - 1] = first_ref[up_z[k]].astype(bf16)
    z_first = [go(fs_ref.at[k - 1], fb_ref.at[k - 1], to_z[k]) for k in range(1, 4)]

    loads[0].wait()
    loads[1].wait()
    for b in range(2 * rows // BLOCK):
        xt_ref[:, BLOCK * b:BLOCK * b + BLOCK] = x_ref[BLOCK * b:BLOCK * b + BLOCK, :].T
    for m in range(0, width, BLOCK):
        g_ref[m:m + BLOCK, :] = mm(xt_ref[m:m + BLOCK, :], d_ref[2])
    half = own_ref.shape[3]
    lane = lax.broadcasted_iota(jnp.int32, (half, 128), 1)
    for p in range(8):
        for n in range(3):
            low = g_ref[2 * half * p:2 * half * p + half, 128 * n:128 * n + 128]
            high = g_ref[2 * half * p + half:2 * half * (p + 1), 128 * n:128 * n + 128]
            own_ref[p % 2, p // 2, n] = jnp.where(lane < 64, low, pltpu.roll(high, 64, 1))
            oth_ref[p % 2, p // 2, n] = jnp.where(lane < 64, pltpu.roll(low, 64, 1), high).astype(bf16)
    y_far = go(oth_ref.at[1 - x], yb_ref.at[0], to_y)
    y_near = go(oth_ref.at[x], yb_ref.at[1], to_y)

    for copy in loads[2:]:
        copy.wait()
    place = lax.broadcasted_iota(jnp.int32, (32, 2 * rows), 1)
    which = lax.broadcasted_iota(jnp.int32, (32, 2 * rows), 0)
    picks = jnp.where((place == pos_ref[:, 0:1]) | (which == 24), 1.0, 0.0).astype(bf16)
    picked = [mm(picks, d_ref[n]) for n in range(3)]
    own_place = lax.broadcasted_iota(jnp.int32, (32, rows), 1) + inner * rows
    own_picks = jnp.where(own_place == pos_ref[:, 0:1], 1.0, 0.0)
    memory = lax.dot_general(own_picks, dr_ref[...], NN, precision=lax.Precision.HIGHEST, preferred_element_type=f32)
    for n in range(3):
        memory = memory + mm(picked[n].astype(bf16), w_ref[n], NT)
    hw = s_ref.shape[2]

    def put(row, value):
        for h in range(2):
            s_ref[h, row:row + 1, :] = value[:, hw * h:hw * h + hw]
    for h in range(2):
        s_ref[h, 0:24, :] = memory[0:24, hw * h:hw * h + hw]
        s_ref[h, 38:40, :] = jnp.zeros((2, hw), f32)
    for n in range(6):
        put(24 + n, jnp.sum(sums_in[n], axis=0, keepdims=True))
    ups = [jnp.sum(up_in[n], axis=0, keepdims=True) for n in (0, 2, 1, 3)]
    total = [value[24:25, :] for value in picked]
    turned = jnp.concatenate([pltpu.roll(picked[2][24:32, 128 * n:128 * n + 128], 64, 1) for n in range(3)], axis=1)[0:1, :]
    for t in range(4):
        n = (t % 2 + inner) % 2 + 2 * ((t // 2 + outer) % 2)
        value = jnp.zeros_like(ups[0])
        for other in range(4):
            value = value + jnp.where(n == other, ups[other], 0.0)
        put(30 + t, value)
        s_ref[0, 34 + t:35 + t, :] = jnp.where(n == 0, total[0], 0.0) + jnp.where(n == 2, total[1], 0.0)
        s_ref[1, 34 + t:35 + t, :] = jnp.where(n == 0, total[2], 0.0) + jnp.where(n == 2, turned, 0.0)
    small = [go(s_ref.at[1 - inner], r_ref.at[0], to_core)]
    hops = [to_y, to_x, near_z, far_z]

    def hop(n):
        small[n].wait_recv()
        t_ref[n] = (s_ref[inner] if n == 0 else t_ref[n - 1]) + r_ref[n]
        if n < 4:
            small.append(go(t_ref.at[n], r_ref.at[n + 1], hops[n]))
        else:
            small.append(go(t_ref.at[n], r_ref.at[5], to_core))
            small_out[inner] = t_ref[n]

    mine = pl.multiple_of(inner * rows, 1024)
    theirs = pl.multiple_of((1 - inner) * rows, 1024)

    def block(start):
        r = pl.ds(pl.multiple_of(start, BLOCK), BLOCK)
        return mm(d_ref[0, r, :], w_ref[0], NT) + mm(d_ref[1, r, :], w_ref[1], NT) + mm(d_ref[2, r, :], w_ref[2], NT)

    def away(b, carry):
        their_ref[pl.ds(pl.multiple_of(b * BLOCK, BLOCK), BLOCK), :] = block(theirs + b * BLOCK).astype(bf16)
        return carry
    lax.fori_loop(0, rows // BLOCK, away, 0)
    tokens = go(their_ref, got_ref, to_core)
    hop(0)
    y_far.wait_recv()
    for k in range(4):
        xs_ref[k] = (own_ref[1 - x, k] + yb_ref[0, k].astype(f32)).astype(bf16)
    x_sum = go(xs_ref, xb_ref, to_x)

    def stay(b, carry):
        tok_ref[pl.ds(pl.multiple_of(b * BLOCK, BLOCK), BLOCK), :] = block(mine + b * BLOCK)
        return carry
    lax.fori_loop(0, rows // BLOCK, stay, 0)
    hop(1)
    y_near.wait_recv()
    x_sum.wait_recv()
    for k in range(4):
        zt_ref[k] = own_ref[x, k] + yb_ref[1, k].astype(f32) + xb_ref[k].astype(f32)
    for k in range(1, 4):
        zs_ref[k - 1] = zt_ref[up_z[k]].astype(bf16)
    z_second = [go(zs_ref.at[k - 1], zb_ref.at[k - 1], to_z[k]) for k in range(1, 4)]
    hop(2)
    tokens.wait_recv()

    def finish(s, carry):
        r = pl.ds(pl.multiple_of(s * STRIP, STRIP), STRIP)
        tok_ref[r, :] = tok_ref[r, :] + got_ref[r, :].astype(f32) + dr_ref[r, :]
        return carry
    lax.fori_loop(0, rows // STRIP, finish, 0)
    out = pltpu.make_async_copy(tok_ref, tok_out, sem.at[8])
    out.start()
    hop(3)
    for copy in z_first:
        copy.wait_recv()
    first_out[...] = first_ref[z] + fb_ref[0].astype(f32) + fb_ref[1].astype(f32) + fb_ref[2].astype(f32)
    for copy in z_second:
        copy.wait_recv()
    second_out[...] = zt_ref[z] + zb_ref[0].astype(f32) + zb_ref[1].astype(f32) + zb_ref[2].astype(f32)
    hop(4)
    small[5].wait_recv()
    small_out[1 - inner] = r_ref[5]
    for copy in started:
        copy.wait_send()
    out.wait()


def leave(x_all, d, w_qkv, third, first, came, dr1, place, sums, up_sums):
    f32, bf16 = jnp.float32, jnp.bfloat16
    rows, width = dr1.shape
    r, half = first.shape[1], first.shape[1] // 2
    shape, v = jax.ShapeDtypeStruct, pltpu.VMEM
    hbm, vmem = pl.BlockSpec(memory_space=pl.ANY), pl.BlockSpec(memory_space=pltpu.VMEM)
    return pl.pallas_call(
        exit_kernel,
        out_shape=(shape((rows, width), f32), shape((r, 384), f32), shape((3, half, 128), f32), shape((2, 40, width // 2), f32)),
        in_specs=[hbm] * 6 + [vmem] * 2 + [hbm] + [vmem] * 3,
        out_specs=[hbm] + [vmem] * 3,
        scratch_shapes=[
            v((2 * rows, width), bf16), v((width, 2 * rows), bf16), v((3, 2 * rows, 384), bf16), v((3, width, 384), bf16),
            v((rows, width), f32), v((width, 384), f32), v((2, 4, 3, half, 128), f32), v((2, 4, 3, half, 128), bf16),
            v((2, 4, 3, half, 128), bf16), v((4, 3, half, 128), bf16), v((4, 3, half, 128), bf16), v((4, 3, half, 128), f32),
            v((3, 3, half, 128), bf16), v((3, 3, half, 128), bf16), v((3, r, 384), bf16), v((3, r, 384), bf16),
            v((rows, width), bf16), v((rows, width), bf16), v((rows, width), f32), v((2, 40, width // 2), f32),
            v((5, 40, width // 2), f32), v((6, 40, width // 2), f32), v((4, r, 384), f32),
            pltpu.SemaphoreType.DMA((16,)), pltpu.SemaphoreType.DMA((16,)), pltpu.SemaphoreType.DMA((9,)),
        ],
        compiler_params=pltpu.CompilerParams(vmem_limit_bytes=VMEM_MAX, collective_id=2, has_side_effects=True),
        cost_estimate=pl.CostEstimate(flops=2 * rows * width * 384 * 8, bytes_accessed=20_000_000, transcendentals=0),
        name="leave",
    )(x_all, *d, w_qkv, third, first, came, dr1, place, sums, up_sums)


def layer_norm(values, norm_gain, norm_shift):
    centre = values - jnp.mean(values, axis=-1, keepdims=True)
    spread = jnp.mean(centre * centre, axis=-1, keepdims=True)
    return centre * lax.rsqrt(spread + EPSILON) * norm_gain + norm_shift


def gelu_exact(values):
    return jax.nn.gelu(values, approximate=False)


AXES = ("dp", "tensor")


class Grid:
    def __init__(self, dp, tensor):
        self.dp, self.tensor = dp, tensor
        factors, rest = [2], dp // 2
        while rest > 8:
            factors.insert(0, 4)
            rest //= 4
        if rest > 1:
            factors.insert(0, rest)
        self.factors = factors

    def digit(self, j):
        stride = 1
        for f in self.factors[j + 1:]:
            stride *= f
        return stride, self.factors[j]

    def my_digit(self, j):
        stride, f = self.digit(j)
        return lax.axis_index("dp") // stride % f

    def turn(self, value, j, k):
        stride, f = self.digit(j)
        pairs = []
        for d in range(self.dp):
            g = d // stride % f
            to = d + ((g + k) % f - g) * stride
            for t in range(self.tensor):
                pairs.append((d * self.tensor + t, to * self.tensor + t))
        return lax.ppermute(value, AXES, pairs)

    def swap_dp(self, value, bit):
        pairs = [(d * self.tensor + t, (d ^ bit) * self.tensor + t) for d in range(self.dp) for t in range(self.tensor)]
        return lax.ppermute(value, AXES, pairs)

    def swap(self, value, bit):
        pairs = [(d * self.tensor + t, d * self.tensor + (t ^ bit)) for d in range(self.dp) for t in range(self.tensor)]
        return lax.ppermute(value, AXES, pairs)

    def gather_stage(self, value, j, axis):
        _, f = self.digit(j)
        g = self.my_digit(j)
        got = [value] + [self.turn(value, j, k) for k in range(1, f)]
        if f == 2:
            lower = jnp.where(g == 0, got[0], got[1])
            upper = jnp.where(g == 0, got[1], got[0])
            return jnp.stack([lower, upper], axis=axis)
        ring = got[::-1]
        return lax.dynamic_slice_in_dim(jnp.stack(ring + ring[:-1], axis=axis), f - 1 - g, f, axis)

    def gather(self, shard, outer_first=False):
        count = len(self.factors)
        value = shard
        for j in range(count - 1):
            value = self.gather_stage(value, j, j)
        if outer_first:
            value = jnp.stack([value, self.swap(value, 2)])
            value = self.gather_stage(value, count - 1, count)
            return value.reshape(2, -1, shard.shape[-1])
        value = self.gather_stage(value, count - 1, count - 1)
        value = value.reshape(-1, shard.shape[-1])
        return jnp.stack([value, self.swap(value, 2)])

    def reduce_stage(self, value, j, axis):
        _, f = self.digit(j)
        g = self.my_digit(j)
        total = lax.dynamic_index_in_dim(value, g, axis, keepdims=False).astype(jnp.float32)
        for k in range(1, f):
            part = lax.dynamic_index_in_dim(value, (g + k) % f, axis, keepdims=False)
            total = total + self.turn(part.astype(jnp.bfloat16), j, k).astype(jnp.float32)
        return total

    def reduce(self, parts, outer_first=True):
        count = len(self.factors)
        columns = parts.shape[-1]
        value = parts
        if outer_first:
            value = value[0].astype(jnp.float32) + self.swap(value[1].astype(jnp.bfloat16), 2).astype(jnp.float32)
            value = value.reshape(*self.factors, -1, columns)
            value = self.reduce_stage(value, count - 1, count - 1)
        else:
            value = value.reshape(2, *self.factors, -1, columns)
            value = self.reduce_stage(value, count - 1, count)
            value = value[0] + self.swap(value[1].astype(jnp.bfloat16), 2).astype(jnp.float32)
        for j in reversed(range(count - 1)):
            value = self.reduce_stage(value, j, j)
        return value

    @property
    def stages(self):
        return len(self.factors) + 1

    def open(self, parts, outer_first):
        columns = parts.shape[-1]
        return parts if outer_first else parts.reshape(2, *self.factors, -1, columns)

    def stage(self, value, outer_first, n):
        count = len(self.factors)
        if n == (0 if outer_first else 1):
            value = value[0].astype(jnp.float32) + self.swap(value[1].astype(jnp.bfloat16), 2).astype(jnp.float32)
            return value.reshape(*self.factors, -1, value.shape[-1]) if outer_first else value
        if n == 0:
            return self.reduce_stage(value, count - 1, count)
        return self.reduce_stage(value, count - n, count - n)

    def total(self, vector):
        for bit in (1, 2):
            vector = vector + self.swap(vector, bit)
        bit = 1
        while bit < self.dp:
            vector = vector + self.swap_dp(vector, bit)
            bit *= 2
        return vector


def shards(grid, tokens, segment_ids, memory_positions, memory_rows, qkv_weight, qv_bias, out_weight, out_bias,
           norm1_gain, norm1_bias, up_weight, up_bias, down_weight, down_bias, norm2_gain, norm2_bias, out_cotangent):
    f32, bf16 = jnp.float32, jnp.bfloat16
    rows, width = tokens.shape
    group_len = segment_ids.shape[1]
    tensor = lax.axis_index("tensor")
    inner, outer = tensor % 2, tensor // 2
    slice_rows = qkv_weight.shape[0]
    heads = qkv_weight.shape[1]
    hd = 64
    hw = heads * hd
    units = up_weight.shape[1]

    segments = lax.dynamic_index_in_dim(segment_ids, outer, 0, keepdims=False)
    positions = lax.dynamic_index_in_dim(memory_positions, outer, 0, keepdims=False)
    row_place = inner * rows + jnp.arange(rows, dtype=jnp.int32)
    picks = (row_place[:, None] == positions[None, :])
    joined = lambda w: w.transpose(1, 0, 2).reshape(width, -1)

    parts = qkv_weight.reshape(slice_rows, heads, 3, hd)
    order_columns = lambda p: jnp.concatenate([p[..., :2, n, :].reshape(*p.shape[:-3], 2 * hd) for n in range(3)]
                                              + [p[..., 2, n, :] for n in range(3)], axis=-1)
    shard_qkv = order_columns(parts)
    shard_out = jnp.pad(out_weight.reshape(slice_rows, hw), ((0, 0), (0, 256 - hw)))
    bias_parts = qv_bias.reshape(heads, 2, hd)
    bias_qkv = order_columns(jnp.stack([bias_parts[:, 0], jnp.zeros_like(bias_parts[:, 0]), bias_parts[:, 1]], 1))
    bias_qkv = jnp.pad(bias_qkv[None], ((0, 15), (0, 64)))
    own_up_bias = jnp.broadcast_to(up_bias[None], (16, units))
    fused = grid.dp == 8 and grid.tensor == 4
    if fused:
        memory = memory_positions.shape[1]
        place = jnp.pad(positions[None], ((0, 7), (0, 32 - memory)), constant_values=-1)
        table = jnp.pad(memory_rows, ((0, 32 - memory), (0, 0)))
        x0, x_all, q, k, v, w_qkv, up_g, down_g, out_g, b_up = entry(tokens, place, table, shard_qkv, bias_qkv, own_up_bias, up_weight, down_weight, shard_out)
        column = jnp.pad(jnp.broadcast_to(positions[:, None], (memory, 128)), ((0, 32 - memory), (0, 0)), constant_values=-1)
        w_qkv = w_qkv.reshape(2, width, 9 * hd)
        third = jnp.concatenate([w_qkv[o][:, (6 + n) * hd:(7 + n) * hd] for n in range(3) for o in range(2)], 1)
        up_all = up_g.reshape(width, units)
        ups = (up_all, grid.swap(up_all, 2))
        down_pair = down_g.reshape(-1, units)
        downs = (down_pair, *[grid.turn(down_pair, 0, k) for k in range(1, 4)])
        outs = (out_g, grid.turn(out_g, 1, 1))
    else:
        x0 = tokens.astype(f32) + jnp.dot(picks.astype(bf16), memory_rows, preferred_element_type=f32)
        xl = x0.astype(bf16)
        w_qkv = grid.gather(shard_qkv)
        other = grid.swap(xl, 1)
        x_all = jnp.concatenate([jnp.where(inner == 0, xl, other), jnp.where(inner == 0, other, xl)])
        b_two = jnp.stack([bias_qkv[0], grid.swap(bias_qkv[0], 2)]).astype(f32)
        y = [(mm(x_all, w_qkv[o]) + b_two[o, :9 * hd]).astype(bf16) for o in range(2)]
        third = lambda n: [one[:, (6 + n) * hd:(7 + n) * hd] for one in y]
        q, k, v = [jnp.concatenate([y[0][:, 2 * n * hd:2 * (n + 1) * hd], y[1][:, 2 * n * hd:2 * (n + 1) * hd]] + third(n), 1)
                   for n in range(3)]
        q = q * jnp.asarray(0.125, bf16)
        b_up = jnp.stack([own_up_bias, grid.swap(own_up_bias, 2)])
        b_up = jnp.concatenate([b_up, grid.swap(b_up, 1)])
        outs, ups, downs = (grid.gather(shard_out, True),), (grid.gather(up_weight),), (grid.gather(down_weight, True),)
    mixed, lse = attend_forward(q, k, v, segments)
    vec = jnp.stack([out_bias, norm1_gain, norm1_bias, down_bias, norm2_gain, norm2_bias, norm2_bias, norm2_bias]).astype(f32)
    (block_out, dr1, do_all, *grads, sums, up_sums) = middle(
        mixed, x0, outs, ups, downs, out_cotangent, vec, b_up)
    if fused:
        return finish_small(grid, tensor, x_all, q, k, v, do_all, mixed, lse, segments, w_qkv, third, dr1, column, sums, up_sums, block_out,
                            grads, hw)
    g_down, g_up, g_out = grads

    TN = (((0,), (0,)), ((), ()))
    tie = lax.optimization_barrier
    kinds = (True, False, True)
    state = [grid.open(parts, kind) for parts, kind in zip((g_down, g_up, g_out), kinds)]
    step = lambda n, state: [grid.stage(value, kind, n) for value, kind in zip(state, kinds)]
    late = [(1, 0, 2)[n] for n in range(3)]
    d = [None] * 3
    state, d[1] = step(0, state), attend_backward(1, q, k, v, do_all, mixed, lse, segments)
    state, d[1], q = tie((state, d[1], q))
    g_one = mm(x_all, d[1], TN).astype(bf16)
    state, d[0] = step(1, state), attend_backward(0, q, k, v, do_all, mixed, lse, segments)
    state, d[0], q, g_one = tie((state, d[0], q, g_one))
    g_zero = mm(x_all, d[0], TN)
    first = g_zero + grid.swap(g_one, 2).astype(f32)
    state, d[2] = step(2, state), attend_backward(2, q, k, v, do_all, mixed, lse, segments)
    state, d[2], first = tie((state, d[2], first))
    for n in range(3, grid.stages):
        state = step(n, state)
    grad_down, grad_up, grad_out = state
    grad_out = grad_out[:, :hw]

    g_two = mm(x_all, d[2], TN)
    side = lambda m, o: jnp.concatenate([m[:, (2 * n + o) * hd:(2 * n + o + 1) * hd] for n in range(3)], 1)
    second = side(g_two, 0) + grid.swap(side(g_two, 1).astype(bf16), 2).astype(f32)
    both = jnp.concatenate([first, second], 1).reshape(*grid.factors, slice_rows, 9 * hd)
    for j in reversed(range(len(grid.factors))):
        both = grid.reduce_stage(both, j, j)
    restore = lambda p: jnp.stack([jnp.concatenate([p[..., 2 * n * hd:2 * (n + 1) * hd].reshape(*p.shape[:-1], 2, hd),
                                                    p[..., None, (6 + n) * hd:(7 + n) * hd]], -2) for n in range(3)], -2)
    grad_qkv = restore(both).reshape(slice_rows, heads, 3 * hd)
    third = jnp.concatenate([w_qkv[o][:, (6 + n) * hd:(7 + n) * hd] for n in range(3) for o in range(2)], 1)
    part = (mm(d[0], w_qkv[0][:, :6 * hd], NT) + mm(d[1], w_qkv[1][:, :6 * hd], NT) + mm(d[2], third, NT)).reshape(2, rows, width)
    mine = lax.dynamic_index_in_dim(part, inner, 0, keepdims=False)
    theirs = lax.dynamic_index_in_dim(part, 1 - inner, 0, keepdims=False).astype(bf16)
    grad_tokens = mine + grid.swap(theirs, 1).astype(f32) + dr1
    d_sum = [jnp.sum(one.astype(f32), axis=0) for one in d]
    d_bias = [jnp.concatenate([d_sum[o]] + [d_sum[2][(2 * n + o) * hd:(2 * n + o + 1) * hd] for n in range(3)]) for o in range(2)]
    dg2, ds2, d_down_bias, dg1, ds1, d_out_bias = jnp.sum(sums, axis=1)
    d_up_bias = jnp.sum(up_sums, axis=1).reshape(2, 2 * units)
    grad_memory = jnp.dot(picks.astype(f32).T, grad_tokens, precision=lax.Precision.HIGHEST)

    order = jnp.arange(4, dtype=jnp.int32) ^ tensor
    up_parts = d_up_bias.reshape(2, 2, units)
    up_parts = jnp.stack([up_parts[0, 0], up_parts[1, 0], up_parts[0, 1], up_parts[1, 1]])[order]
    take = lambda o: restore(d_bias[o])[:, 0::2].reshape(-1)
    blank = jnp.zeros((2 * hw,), f32)
    qv_parts = jnp.stack([take(0), blank, take(1), blank])[order]
    pieces = [grad_memory.reshape(-1), d_out_bias, dg1, ds1, d_down_bias, dg2, ds2, up_parts.reshape(-1), qv_parts.reshape(-1)]
    summed = grid.total(jnp.concatenate(pieces))
    outs, at = [], 0
    for piece in pieces:
        outs.append(lax.slice_in_dim(summed, at, at + piece.size))
        at += piece.size
    t_memory, t_out_bias, t_g1, t_s1, t_down_bias, t_g2, t_s2, t_up, t_qv = outs
    grad_up_bias = lax.dynamic_index_in_dim(t_up.reshape(4, units), tensor, 0, keepdims=False)
    grad_qv = lax.dynamic_index_in_dim(t_qv.reshape(4, heads, 2 * hd), tensor, 0, keepdims=False)
    return (block_out, grad_tokens, t_memory.reshape(-1, width), grad_qkv, grad_qv,
            grad_out.reshape(slice_rows, heads, hd), t_out_bias, t_g1, t_s1, grad_up, grad_up_bias, grad_down,
            t_down_bias, t_g2, t_s2)


def blend_one_kernel(x_ref, down, down_early, down_late, up, up_in, out, out_in, kept_down, kept_up, kept_out, send_x, send_y):
    f32, bf16 = jnp.float32, jnp.bfloat16
    x = x_ref[0]
    width = down.shape[-1]
    add = lambda a, b: a.astype(f32) + b.astype(f32)
    early = pl.program_id(0) < pl.num_programs(0) // 2
    down_in = lambda n: jnp.where(early, down_early[0, n], down_late[0, n])
    kept_down[0] = add(down[0, x], down_in(x))
    kept_out[0] = add(out[0, x], out_in[0, x])
    send_x[0, :, 0:width] = add(down[0, 1 - x], down_in(1 - x)).astype(bf16)
    send_x[0, :, width:] = add(out[0, 1 - x], out_in[0, 1 - x]).astype(bf16)
    kept_up[0] = add(up[0, 0], up_in[0, 0])
    send_y[0] = add(up[1, 0], up_in[1, 0]).astype(bf16)


def blend_one(x, down, down_early, down_late, up, up_in, out, out_in):
    f32, bf16 = jnp.float32, jnp.bfloat16
    _, zs, r, width = up.shape
    ow = out.shape[-1]
    shape = jax.ShapeDtypeStruct
    by_x = lambda columns: pl.BlockSpec((1, 2, r, columns), lambda j, *_: (j, 0, 0, 0))
    by_y = pl.BlockSpec((2, 1, r, width), lambda j, *_: (0, j, 0, 0))
    one = lambda columns: pl.BlockSpec((1, r, columns), lambda j, *_: (j, 0, 0))
    lower = pl.BlockSpec((1, 2, r, width), lambda j, *_: (jnp.minimum(j, zs // 2 - 1), 0, 0, 0))
    upper = pl.BlockSpec((1, 2, r, width), lambda j, *_: (jnp.maximum(j - zs // 2, 0), 0, 0, 0))
    fold = lambda a: a.reshape(-1, 2, r, a.shape[-1])
    return pl.pallas_call(
        blend_one_kernel,
        out_shape=(shape((zs, r, width), f32), shape((zs, r, width), f32), shape((zs, r, ow), f32),
                   shape((zs, r, width + ow), bf16), shape((zs, r, width), bf16)),
        grid_spec=pltpu.PrefetchScalarGridSpec(
            num_scalar_prefetch=1, grid=(zs,),
            in_specs=[by_x(width), lower, upper, by_y, by_y, by_x(ow), by_x(ow)],
            out_specs=[one(width), one(width), one(ow), one(width + ow), one(width)]),
        compiler_params=pltpu.CompilerParams(dimension_semantics=("arbitrary",), vmem_limit_bytes=VMEM_MAX),
        cost_estimate=pl.CostEstimate(flops=8 * zs * r * width, bytes_accessed=10_000_000, transcendentals=0),
        name="blend_one",
    )(x.reshape(1), fold(down), fold(down_early), fold(down_late), up, up_in, fold(out), fold(out_in))


def blend_two_kernel(at_ref, kept_down, kept_up, kept_out, came_x, came_y, first, kept_z, kept_first, *sends):
    f32, bf16 = jnp.float32, jnp.bfloat16
    x, z = at_ref[0], at_ref[1]
    zs, r, width = kept_down.shape
    for k in range(zs):
        n = (z + k) % zs
        parts = (kept_down[n] + came_x[n, :, 0:width].astype(f32), kept_up[n] + came_y[n].astype(f32),
                 kept_out[n] + came_x[n, :, width:].astype(f32))
        start = 0
        for part in parts:
            stop = start + part.shape[1]
            if k == 0:
                kept_z[:, start:stop] = part
            else:
                sends[k - 1][:, start:stop] = part.astype(bf16)
            start = stop
        kept_first[k] = first[k, x]
        sends[zs - 1][k] = first[k, 1 - x].astype(bf16)


def blend_two(x, z, kept_down, kept_up, kept_out, came_x, came_y, first):
    f32, bf16 = jnp.float32, jnp.bfloat16
    zs, r, width = kept_down.shape
    columns = 2 * width + kept_out.shape[-1]
    shape = jax.ShapeDtypeStruct
    vmem = pl.BlockSpec(memory_space=pltpu.VMEM)
    return pl.pallas_call(
        blend_two_kernel,
        out_shape=(shape((r, columns), f32), shape((zs, r, first.shape[-1]), f32), *[shape((r, columns), bf16)] * (zs - 1),
                   shape((zs, r, first.shape[-1]), bf16)),
        in_specs=[pl.BlockSpec(memory_space=pltpu.SMEM)] + [vmem] * 6,
        out_specs=[vmem] * (zs + 2),
        compiler_params=pltpu.CompilerParams(vmem_limit_bytes=VMEM_MAX),
        cost_estimate=pl.CostEstimate(flops=4 * zs * r * columns, bytes_accessed=10_000_000, transcendentals=0),
        name="blend_two",
    )(jnp.stack([x, z]), kept_down, kept_up, kept_out, came_x, came_y, first.reshape(zs, 2, r, first.shape[-1]))


def spread_kernel(t_ref, kept, came_one, came_two, came_three, small, down, up, out, memory, vec, up_bias, qv):
    f32 = jnp.float32
    width = down.shape[1]
    for ref, start in ((down, 0), (up, width), (out, 2 * width)):
        cols = slice(start, start + ref.shape[1])
        ref[...] = (kept[:, cols] + came_one[:, cols].astype(f32)) + (came_two[:, cols].astype(f32) + came_three[:, cols].astype(f32))
    half = width // 2
    t = t_ref[0]
    for h in range(2):
        cols = slice(half * h, half * h + half)
        memory[:, cols] = small[h, 0:memory.shape[0], :]
        vec[:, cols] = small[h, 24:32, :]
        up_bias[:, cols] = small[h, pl.ds(30 + t, 1), :]
        qv[h:h + 1, :] = small[h, pl.ds(34 + t, 1), :]


def spread(tensor, kept, came, small, memory, ow):
    f32 = jnp.float32
    r, columns = kept.shape
    width = 2 * small.shape[2]
    shape = jax.ShapeDtypeStruct
    vmem = pl.BlockSpec(memory_space=pltpu.VMEM)
    return pl.pallas_call(
        spread_kernel,
        out_shape=(shape((r, width), f32), shape((r, width), f32), shape((r, ow), f32), shape((memory, width), f32),
                   shape((8, width), f32), shape((1, width), f32), shape((2, width // 2), f32)),
        in_specs=[pl.BlockSpec(memory_space=pltpu.SMEM)] + [vmem] * 5,
        out_specs=[vmem] * 7,
        compiler_params=pltpu.CompilerParams(vmem_limit_bytes=VMEM_MAX),
        cost_estimate=pl.CostEstimate(flops=3 * r * columns, bytes_accessed=3_000_000, transcendentals=0),
        name="spread",
    )(tensor.reshape(1), kept, *came, small)


def finish_small(grid, tensor, x_all, q, k, v, do_all, mixed, lse, segments, w_qkv, third, dr1, column, sums, up_sums, block_out,
                 grads, hw):
    f32, bf16 = jnp.float32, jnp.bfloat16
    tie = lax.optimization_barrier
    TN = (((0,), (0,)), ((), ()))
    width = dr1.shape[1]
    x, z = lax.axis_index("dp") % 2, lax.axis_index("dp") // 2
    down, down_far, down_early, up, up_far, out, out_far = grads

    def beside(pair, q, sends):
        arrays, q = tie(([a for a, _ in sends], q))
        came = [move(a) for a, (_, move) in zip(arrays, sends)]
        d = attend_backward(pair, q, k, v, do_all, mixed, lse, segments)
        return tie((came, d, q))

    over_y = lambda a: grid.swap(a, 2)
    over_x = lambda a: grid.turn(a, 1, 1)
    (down_in, out_in, up_in), d_one, q = beside(1, q, [(down_far, over_y), (out_far, over_y), (up_far, over_x)])
    g_one = mm(x_all, d_one, TN).astype(bf16)
    kept_down, kept_up, kept_out, send_x, send_y = blend_one(x, down, down_early, down_in, up, up_in, out, out_in)
    (came_x, came_y, came_one), d_zero, q = beside(0, q, [(send_x, over_x), (send_y, over_y), (g_one, over_y)])
    first = mm(x_all, d_zero, TN) + came_one.astype(f32)
    kept, kept_first, *sends = blend_two(x, z, kept_down, kept_up, kept_out, came_x, came_y, first)
    over_z = [lambda a, n=n: grid.turn(a, 0, n) for n in range(1, 4)]
    came, d_two, q = beside(2, q, list(zip(sends, over_z + [over_x])))
    grad_tokens, one, two, small = leave(x_all, (d_zero, d_one, d_two), w_qkv, third, kept_first, came[3], dr1, column, sums, up_sums)
    grad_down, grad_up, grad_out, grad_memory, vec, up_bias, qv = spread(tensor, kept, came[:3], small, 20, out.shape[-1])
    hd = 64
    slice_rows = one.shape[0]
    two = two.reshape(3, slice_rows // 2, 2, hd).transpose(2, 1, 0, 3).reshape(slice_rows, 1, 3, hd)
    grad_qkv = jnp.concatenate([one.reshape(slice_rows, 3, 2, hd).transpose(0, 2, 1, 3), two], 1).reshape(slice_rows, 3, 3 * hd)
    part = lambda n: jnp.concatenate([qv[0, 128 * n:128 * n + 128].reshape(2, hd), qv[1:2, 128 * n:128 * n + hd]])
    grad_qv = jnp.concatenate([part(0), part(2)], 1)
    t_out_bias, t_g1, t_s1, t_down_bias, t_g2, t_s2 = [vec[n] for n in (5, 3, 4, 2, 0, 1)]
    return (block_out, grad_tokens, grad_memory, grad_qkv, grad_qv,
            grad_out[:, :hw].reshape(slice_rows, 3, hd), t_out_bias, t_g1, t_s1, grad_up, up_bias.reshape(width), grad_down,
            t_down_bias, t_g2, t_s2)


def solution(mesh):
    grid = Grid(mesh.shape["dp"], mesh.shape["tensor"])
    tokens, dp, none = P(AXES, None), P("dp", None), P()
    heads, matrix = P("dp", "tensor", None), P("dp", "tensor")
    in_specs = (tokens, dp, dp, none, heads, P("tensor", None), heads, none, none, none, matrix, P("tensor"), matrix,
                none, none, none, tokens)
    out_specs = (tokens, tokens, none, heads, P("tensor", None), heads, none, none, none, matrix, P("tensor"), matrix,
                 none, none, none)

    def run(*args):
        return shards(grid, *args)

    return jax.shard_map(run, mesh=mesh, in_specs=in_specs, out_specs=out_specs, check_vma=False)
```

profile of v0, /device:TPU:0, one launch (start us, length us, event | category | flops | bytes accessed | tf_op | source)
XLA Modules:
  0.0 346.0 jit_solution(1242676992118792259)
XLA Ops:
  0.7 1.1 copy.36
  1.8 0.8 reshape.99
  2.6 0.7 constant_dynamic-slice_fusion
  4.7 1.4 pad.23.mem_ref
  6.8 0.9 copy.43
  7.7 0.6 pad.25.wo_ref
  8.4 0.7 concatenate.26.wq_ref
  9.1 1.3 broadcast_in_dim.11.bu_ref
  10.4 46.3 %entry.1 = (f32[1024,768]{1,0:T(8,128)}, bf16[2048,768]{1,0:T(8,128)(2,1)}, bf16[2048,384]{1,0:T(8,128)(2,1)}, bf16[2048,384]{1,0:T(8,128)(2,1)}, bf16[2048,384]...) custom-call(bf16[1024,768]{1,0:T(8,128)(2,1)} %tokens.1, ...), custom_call_target="tpu_custom_call" | custom-call | flops 3623878656 | bytes 20000000 | tf_op jit(solution)/shard_map/entry/pallas_call | solution.py:768
  56.7 1.1 collective-permute-start.1
  58.3 4.4 %collective-permute-start.3 = (bf16[192,768]{1,0:T(8,128)(2,1)}, bf16[192,768]{1,0:T(8,128)(2,1)}, u32[]{:S(2)}, u32[]{:S(2)}) collective-permute-start(bf16[192,768]{1,0:T(8,128)(2,1)} %bitcast.70), channel_id=1, source_target_pairs={{0,16},{1,17},{2,18},{3,19},{4,20},{5,21},{6,22},{7,23},{8,24},{9,... | collective-permute-start | bytes 884744 | tf_op jit(solution)/shard_map/ppermute | solution.py:1010
  65.1 1.3 broadcast_in_dim.12.kseg_ref
  66.4 0.6 broadcast_in_dim.13.qseg_ref
  67.0 37.4 %attend_forward.1 = (bf16[2048,384]{1,0:T(8,128)(2,1)}, f32[8,2048]{1,0:T(8,128)}) custom-call(s32[8]{0:T(128)} %slice.111.first_ref, s32[8]{0:T(128)} %slice.112.last_ref, bf16[2048,384]{1,0:T(8,128)(2,1)} %get-tuple-element.140.q_ref, bf16[2048,384]{1,0:T(8,128)(2,1)} %get-tuple-element.90.k_ref, bf16[2048,384]{1,0:T(8,128)(2,1)} %get-tuple-element.91.v_ref, ...), custom_call_target="tpu_custom_call" | custom-call | flops 6442450944 | bytes 6291456 | tf_op jit(solution)/shard_map/attend_forward/pallas_call | solution.py:106
  104.6 0.6 convert_element_type.15.refs_9_
  105.3 84.2 %middle.1 = (bf16[1024,768]{1,0:T(8,128)(2,1)}, f32[1024,768]{1,0:T(8,128)}, bf16[2048,384]{1,0:T(8,128)(2,1)}, bf16[768,768]{1,0:T(8,128)(2,1)}, bf16[384,768]{...) custom-call(bf16[2048,384]{1,0:T(8,128)(2,1)} %get-tuple-element.92., ...), custom_call_target="tpu_custom_call" | custom-call | flops 32614907904 | bytes 60000000 | tf_op jit(solution)/shard_map/middle/pallas_call | solution.py:584
  190.1 2.9 fusion
  193.0 2.5 collective-permute-start.5
  195.6 23.1 %attend_backward.3.d1 = bf16[2048,384]{1,0:T(8,128)(2,1)} custom-call(s32[8]{0:T(128)} %slice.111.first_ref, s32[8]{0:T(128)} %slice.112.last_ref, bf16[2048,384]{1,0:T(8,128)(2,1)} %get-tuple-element.140.q_ref, bf16[2048,384]{1,0:T(8,128)(2,1)} %get-tuple-element.109.do_ref, bf16[2048,384]{1,0:T(8,128)(2,1)} %get-tuple-element.92.o_all.o_ref, ...), custom_call_target="tpu_custom_call" | custom-call | flops 5368709120 | bytes 3670016 | tf_op jit(solution)/shard_map/attend_backward/pallas_call | solution.py:210
  218.7 5.0 %convolution_convert_fusion = bf16[768,384]{1,0:T(8,128)(2,1)} fusion(bf16[2048,768]{1,0:T(8,128)(2,1)} %get-tuple-element.99.x_all, bf16[2048,384]{1,0:T(8,128)(2,1)} %attend_backward.3.d1), kind=kOutput, calls=%fused_computation.1 | convolution fusion | flops 1208254464 | bytes 5308416 | tf_op jit(solution)/shard_map/dot_general | solution.py:19
  223.8 5.0 %blend_one.1 = (f32[4,96,768]{2,1,0:T(8,128)}, f32[4,96,768]{2,1,0:T(8,128)}, f32[4,96,256]{2,1,0:T(8,128)}, bf16[4,96,1024]{2,1,0:T(8,128)(2,1)}, bf16[4,96,768]{2,1,0:T(8,128)(2,1)}) custom-call(s32[1]{0:T(128)} %bitcast.13.x_ref, bf16[4,2,96,768]{3,2,1,0:T(8,128)(2,1)} %bitcast.46, bf16[2,2,96,768]{3,2,1,0:T(8,128)(2,1)} %bitcast.52, ...), custom_call_target="tpu_custom_call" | custom-call | flops 2359296 | bytes 10000000 | tf_op jit(solution)/shard_map/blend_one/pallas_call | solution.py:1249
  228.7 3.0 collective-permute-start.8
  231.8 1.6 fusion.1
  233.3 1.2 concatenate.28.third
  234.5 1.0 collective-permute-start.9
  235.5 1.0 collective-permute-start.10
  237.1 22.8 %attend_backward.4.d0 = bf16[2048,384]{1,0:T(8,128)(2,1)} custom-call(s32[8]{0:T(128)} %slice.111.first_ref, s32[8]{0:T(128)} %slice.112.last_ref, bf16[2048,384]{1,0:T(8,128)(2,1)} %get-tuple-element.140.q_ref, bf16[2048,384]{1,0:T(8,128)(2,1)} %get-tuple-element.109.do_ref, bf16[2048,384]{1,0:T(8,128)(2,1)} %get-tuple-element.92.o_all.o_ref, ...), custom_call_target="tpu_custom_call" | custom-call | flops 5368709120 | bytes 3670016 | tf_op jit(solution)/shard_map/attend_backward/pallas_call | solution.py:210
  260.0 1.5 collective-permute-done.10
  261.5 5.3 %convolution_add_fusion = f32[768,384]{1,0:T(8,128)} fusion(bf16[2048,768]{1,0:T(8,128)(2,1)} %get-tuple-element.99.x_all, bf16[2048,384]{1,0:T(8,128)(2,1)} %attend_backward.4.d0, bf16[768,384]{1,0:T(8,128)(2,1)} %collective-permute-done.10), kind=kOutput, calls=%fused_computation | convolution fusion | flops 1208549376 | bytes 6488064 | tf_op jit(solution)/shard_map/dot_general | solution.py:19
  266.9 4.3 %blend_two.1 = (f32[96,1792]{1,0:T(8,128)}, f32[4,96,384]{2,1,0:T(8,128)}, bf16[96,1792]{1,0:T(8,128)(2,1)}, bf16[96,1792]{1,0:T(8,128)(2,1)}, bf16[96,1792]{1,0:T(8,128)(2,1)}, /*index=5*/bf16[4,96,384]{2,1,0:T(8,128)(2,1)}) custom-call(s32[2]{0:T(128)} %pad_add_fusion.at_ref, f32[4,96,768]{2,1,0:T(8,128)} %get-tuple-element.125.kept_down, ...), custom_call_target="tpu_custom_call" | custom-call | flops 2752512 | bytes 10000000 | tf_op jit(solution)/shard_map/blend_two/pallas_call | solution.py:1289
  271.1 1.9 collective-permute-start.11
  273.1 2.4 collective-permute-start.13
  275.5 1.4 collective-permute-start.14
  276.9 23.2 %attend_backward.5.d2 = bf16[2048,384]{1,0:T(8,128)(2,1)} custom-call(s32[8]{0:T(128)} %slice.111.first_ref, s32[8]{0:T(128)} %slice.112.last_ref, bf16[2048,384]{1,0:T(8,128)(2,1)} %get-tuple-element.140.q_ref, bf16[2048,384]{1,0:T(8,128)(2,1)} %get-tuple-element.109.do_ref, bf16[2048,384]{1,0:T(8,128)(2,1)} %get-tuple-element.92.o_all.o_ref, ...), custom_call_target="tpu_custom_call" | custom-call | flops 5368709120 | bytes 3670016 | tf_op jit(solution)/shard_map/attend_backward/pallas_call | solution.py:210
  300.2 0.7 pad.27.pos_ref
  300.8 30.6 %leave.1 = (f32[1024,768]{1,0:T(8,128)}, f32[96,384]{1,0:T(8,128)}, f32[3,48,128]{2,1,0:T(8,128)}, f32[2,40,384]{2,1,0:T(8,128)}) custom-call(bf16[2048,768]{1,0:T(8,128)(2,1)} %get-tuple-element.99.x_all, bf16[2048,384]{1,0:T(8,128)(2,1)} %attend_backward.4.d0, bf16[2048,384]{1,0:T(8,128)(2,1)} %attend_backward.3.d1, bf16[2048,384]{1,0:T(8,128)(2,1)} %attend_backward.5.d2, ...), custom_call_target="tpu_custom_call" | custom-call | flops 4831838208 | bytes 20000000 | tf_op jit(solution)/shard_map/leave/pallas_call | solution.py:948
  331.5 2.3 spread.1
  333.8 0.7 fusion.5
  334.5 0.7 slice_reduce_fusion.9
  335.3 1.0 reshape.113
  336.7 1.1 copy.44
  337.9 0.9 copy.49
  338.9 0.7 copy.48
  339.7 0.6 slice_reduce_fusion
  340.9 0.7 maximum_maximum_fusion
  341.6 1.1 copy.57
  342.7 1.3 copy-done.2
  344.0 1.7 copy.58
  (86 shorter events, 7.6 us)
Async XLA Ops:
  0.6 63.2 %copy-start = (s32[2,2048]{1,0:T(2,128)S(1)}, s32[2,2048]{1,0:T(2,128)}, u32[]{:S(2)}) copy-start(s32[2,2048]{1,0:T(2,128)} %param.18) | copy-start | bytes 49156
  56.7 48.6 %collective-permute-start.1 = (bf16[768,768]{1,0:T(8,128)(2,1)}, bf16[768,768]{1,0:T(8,128)(2,1)}, u32[]{:S(2)}, u32[]{:S(2)}) collective-permute-start(bf16[768,768]{1,0:T(8,128)(2,1)} %bitcast.67), channel_id=1, source_target_pairs={{0,2},{1,3},{2,0},{3,1},{4,6},{5,7},{6,4},{7,5},{8,10},{9,11},{10,... | collective-permute-start | bytes 3538952 | tf_op jit(solution)/shard_map/ppermute | solution.py:1018
  57.8 47.5 %collective-permute-start.2 = (bf16[192,768]{1,0:T(8,128)(2,1)}, bf16[192,768]{1,0:T(8,128)(2,1)}, u32[]{:S(2)}, u32[]{:S(2)}) collective-permute-start(bf16[192,768]{1,0:T(8,128)(2,1)} %bitcast.69), channel_id=1, source_target_pairs={{0,8},{1,9},{2,10},{3,11},{4,12},{5,13},{6,14},{7,15},{8,16},{9,17... | collective-permute-start | bytes 884744 | tf_op jit(solution)/shard_map/ppermute | solution.py:1010
  58.3 46.9 %collective-permute-start.3 = (bf16[192,768]{1,0:T(8,128)(2,1)}, bf16[192,768]{1,0:T(8,128)(2,1)}, u32[]{:S(2)}, u32[]{:S(2)}) collective-permute-start(bf16[192,768]{1,0:T(8,128)(2,1)} %bitcast.70), channel_id=1, source_target_pairs={{0,16},{1,17},{2,18},{3,19},{4,20},{5,21},{6,22},{7,23},{8,24},{9,... | collective-permute-start | bytes 884744 | tf_op jit(solution)/shard_map/ppermute | solution.py:1010
  62.7 42.5 %collective-permute-start.4 = (bf16[192,768]{1,0:T(8,128)(2,1)}, bf16[192,768]{1,0:T(8,128)(2,1)}, u32[]{:S(2)}, u32[]{:S(2)}) collective-permute-start(bf16[192,768]{1,0:T(8,128)(2,1)} %bitcast.71), channel_id=1, source_target_pairs={{0,24},{1,25},{2,26},{3,27},{4,28},{5,29},{6,30},{7,31},{8,0},{9,1... | collective-permute-start | bytes 884744 | tf_op jit(solution)/shard_map/ppermute | solution.py:1010
  63.2 42.0 %collective-permute-start = (bf16[2,4,96,256]{3,2,1,0:T(8,128)(2,1)}, bf16[2,4,96,256]{3,2,1,0:T(8,128)(2,1)}, u32[]{:S(2)}, u32[]{:S(2)}) collective-permute-start(bf16[2,4,96,256]{3,2,1,0:T(8,128)(2,1)} %get-tuple-element.94.refs_0_), channel_id=1, source_target_pairs={{0,4},{1,5},{2,6},{3,7},{4,0},{5,1},{6,2},{7,3},{8,12},{9,13},{10,... | collective-permute-start | bytes 1179656 | tf_op jit(solution)/shard_map/ppermute | solution.py:1010
  67.0 37.4 %copy-start.7 = (bf16[768]{0:T(1024)(128)(2,1)S(1)}, bf16[768]{0:T(1024)(128)(2,1)}, u32[]{:S(2)}) copy-start(bf16[768]{0:T(1024)(128)(2,1)} %param.24) | copy-start | bytes 4612
  67.0 37.4 %copy-start.8 = (bf16[768]{0:T(1024)(128)(2,1)S(1)}, bf16[768]{0:T(1024)(128)(2,1)}, u32[]{:S(2)}) copy-start(bf16[768]{0:T(1024)(128)(2,1)} %param.25) | copy-start | bytes 4612
  67.0 37.5 %copy-start.9 = (bf16[768]{0:T(1024)(128)(2,1)S(1)}, bf16[768]{0:T(1024)(128)(2,1)}, u32[]{:S(2)}) copy-start(bf16[768]{0:T(1024)(128)(2,1)} %param.26) | copy-start | bytes 4612
  67.0 37.5 %copy-start.10 = (bf16[768]{0:T(1024)(128)(2,1)S(1)}, bf16[768]{0:T(1024)(128)(2,1)}, u32[]{:S(2)}) copy-start(bf16[768]{0:T(1024)(128)(2,1)} %param.30) | copy-start | bytes 4612
  67.0 37.5 %copy-start.11 = (bf16[768]{0:T(1024)(128)(2,1)S(1)}, bf16[768]{0:T(1024)(128)(2,1)}, u32[]{:S(2)}) copy-start(bf16[768]{0:T(1024)(128)(2,1)} %param.31) | copy-start | bytes 4612
  67.0 37.5 %copy-start.12 = (bf16[768]{0:T(1024)(128)(2,1)S(1)}, bf16[768]{0:T(1024)(128)(2,1)}, u32[]{:S(2)}) copy-start(bf16[768]{0:T(1024)(128)(2,1)} %param.32) | copy-start | bytes 4612
  189.5 29.2 %collective-permute-start.7 = (bf16[2,4,96,768]{3,2,1,0:T(8,128)(2,1)}, bf16[2,4,96,768]{3,2,1,0:T(8,128)(2,1)}, u32[]{:S(2)}, u32[]{:S(2)}) collective-permute-start(bf16[2,4,96,768]{3,2,1,0:T(8,128)(2,1)} %get-tuple-element.107), channel_id=1, source_target_pairs={{0,4},{1,5},{2,6},{3,7},{4,0},{5,1},{6,2},{7,3},{8,12},{9,13},{10,... | collective-permute-start | bytes 3538952 | tf_op jit(solution)/shard_map/ppermute | solution.py:1010
  190.1 5.4 %copy-start.13 = (s32[2,20]{1,0:T(2,128)S(1)}, s32[2,20]{1,0:T(2,128)}, u32[]{:S(2)}) copy-start(s32[2,20]{1,0:T(2,128)} %param.19) | copy-start | bytes 484
  193.0 25.7 %collective-permute-start.5 = (bf16[384,768]{1,0:T(8,128)(2,1)}, bf16[384,768]{1,0:T(8,128)(2,1)}, u32[]{:S(2)}, u32[]{:S(2)}) collective-permute-start(bf16[384,768]{1,0:T(8,128)(2,1)} %get-tuple-element.105), channel_id=1, source_target_pairs={{0,2},{1,3},{2,0},{3,1},{4,6},{5,7},{6,4},{7,5},{8,10},{9,11},{10,... | collective-permute-start | bytes 1769480 | tf_op jit(solution)/shard_map/ppermute | solution.py:1018
  195.5 23.2 %collective-permute-start.6 = (bf16[768,256]{1,0:T(8,128)(2,1)}, bf16[768,256]{1,0:T(8,128)(2,1)}, u32[]{:S(2)}, u32[]{:S(2)}) collective-permute-start(bf16[768,256]{1,0:T(8,128)(2,1)} %get-tuple-element.106), channel_id=1, source_target_pairs={{0,2},{1,3},{2,0},{3,1},{4,6},{5,7},{6,4},{7,5},{8,10},{9,11},{10,... | collective-permute-start | bytes 1179656 | tf_op jit(solution)/shard_map/ppermute | solution.py:1018
  228.7 32.8 %collective-permute-start.8 = (bf16[4,96,1024]{2,1,0:T(8,128)(2,1)}, bf16[4,96,1024]{2,1,0:T(8,128)(2,1)}, u32[]{:S(2)}, u32[]{:S(2)}) collective-permute-start(bf16[4,96,1024]{2,1,0:T(8,128)(2,1)} %get-tuple-element.120), channel_id=1, source_target_pairs={{0,4},{1,5},{2,6},{3,7},{4,0},{5,1},{6,2},{7,3},{8,12},{9,13},{10,... | collective-permute-start | bytes 2359304 | tf_op jit(solution)/shard_map/ppermute | solution.py:1010
  234.5 25.4 %collective-permute-start.9 = (bf16[4,96,768]{2,1,0:T(8,128)(2,1)}, bf16[4,96,768]{2,1,0:T(8,128)(2,1)}, u32[]{:S(2)}, u32[]{:S(2)}) collective-permute-start(bf16[4,96,768]{2,1,0:T(8,128)(2,1)} %get-tuple-element.121), channel_id=1, source_target_pairs={{0,2},{1,3},{2,0},{3,1},{4,6},{5,7},{6,4},{7,5},{8,10},{9,11},{10,... | collective-permute-start | bytes 1769480 | tf_op jit(solution)/shard_map/ppermute | solution.py:1018
  235.5 26.0 %collective-permute-start.10 = (bf16[768,384]{1,0:T(8,128)(2,1)}, bf16[768,384]{1,0:T(8,128)(2,1)}, u32[]{:S(2)}, u32[]{:S(2)}) collective-permute-start(bf16[768,384]{1,0:T(8,128)(2,1)} %convolution_convert_fusion), channel_id=1, source_target_pairs={{0,2},{1,3},{2,0},{3,1},{4,6},{5,7},{6,4},{7,5},{8,10},{9,11},{10,... | collective-permute-start | bytes 1769480 | tf_op jit(solution)/shard_map/ppermute | solution.py:1018
  271.1 29.0 %collective-permute-start.11 = (bf16[96,1792]{1,0:T(8,128)(2,1)}, bf16[96,1792]{1,0:T(8,128)(2,1)}, u32[]{:S(2)}, u32[]{:S(2)}) collective-permute-start(bf16[96,1792]{1,0:T(8,128)(2,1)} %get-tuple-element.136), channel_id=1, source_target_pairs={{0,8},{1,9},{2,10},{3,11},{4,12},{5,13},{6,14},{7,15},{8,16},{9,17... | collective-permute-start | bytes 1032200 | tf_op jit(solution)/shard_map/ppermute | solution.py:1010
  273.1 27.1 %collective-permute-start.12 = (bf16[96,1792]{1,0:T(8,128)(2,1)}, bf16[96,1792]{1,0:T(8,128)(2,1)}, u32[]{:S(2)}, u32[]{:S(2)}) collective-permute-start(bf16[96,1792]{1,0:T(8,128)(2,1)} %get-tuple-element.137), channel_id=1, source_target_pairs={{0,16},{1,17},{2,18},{3,19},{4,20},{5,21},{6,22},{7,23},{8,24},{9,... | collective-permute-start | bytes 1032200 | tf_op jit(solution)/shard_map/ppermute | solution.py:1010
  273.1 27.1 %collective-permute-start.13 = (bf16[96,1792]{1,0:T(8,128)(2,1)}, bf16[96,1792]{1,0:T(8,128)(2,1)}, u32[]{:S(2)}, u32[]{:S(2)}) collective-permute-start(bf16[96,1792]{1,0:T(8,128)(2,1)} %get-tuple-element.138), channel_id=1, source_target_pairs={{0,24},{1,25},{2,26},{3,27},{4,28},{5,29},{6,30},{7,31},{8,0},{9,1... | collective-permute-start | bytes 1032200 | tf_op jit(solution)/shard_map/ppermute | solution.py:1010
  275.5 24.6 %collective-permute-start.14 = (bf16[4,96,384]{2,1,0:T(8,128)(2,1)}, bf16[4,96,384]{2,1,0:T(8,128)(2,1)}, u32[]{:S(2)}, u32[]{:S(2)}) collective-permute-start(bf16[4,96,384]{2,1,0:T(8,128)(2,1)} %get-tuple-element.139), channel_id=1, source_target_pairs={{0,4},{1,5},{2,6},{3,7},{4,0},{5,1},{6,2},{7,3},{8,12},{9,13},{10,... | collective-permute-start | bytes 884744 | tf_op jit(solution)/shard_map/ppermute | solution.py:1010
  333.8 5.1 %copy-start.4 = (f32[96,256]{1,0:T(8,128)S(1)}, f32[96,256]{1,0:T(8,128)}, u32[]{:S(2)}) copy-start(f32[96,256]{1,0:T(8,128)} %get-tuple-element.158) | copy-start | bytes 294916
  335.3 4.4 %copy-start.5 = (f32[8,768]{1,0:T(8,128)S(1)}, f32[8,768]{1,0:T(8,128)}, u32[]{:S(2)}) copy-start(f32[8,768]{1,0:T(8,128)} %get-tuple-element.159) | copy-start | bytes 73732
  335.3 5.0 %copy-start.6 = (f32[1,768]{1,0:T(1,128)S(1)}, f32[1,768]{1,0:T(1,128)}, u32[]{:S(2)}) copy-start(f32[1,768]{1,0:T(1,128)} %get-tuple-element.161) | copy-start | bytes 9220
  336.3 5.3 %copy-start.3 = (bf16[1024,768]{1,0:T(8,128)(2,1)S(1)}, bf16[1024,768]{1,0:T(8,128)(2,1)}, u32[]{:S(2)}) copy-start(bf16[1024,768]{1,0:T(8,128)(2,1)} %get-tuple-element.239) | copy-start | bytes 4718596
  341.6 2.5 copy-start.2
  344.0 1.7 copy-start.1
where the time goes:
time: 349 us; the launch traced here: 346 us
  Pallas kernels  279 us (80%)
  local copies, waits for them, and re-layouts  29.8 us (9%)
  starting transfers between devices  21.2 us (6%)
  matrix products  10.4 us (3%)
    pallas_call x1, Pallas kernels, middle(): pl.pallas_call(kernel, out_shape=(shape((rows, width), bf16), shape((rows...  84.2 us
    pallas_call x3, Pallas kernels, attend_backward(): pl.pallas_call(functools.partial(backward_kernel, 2 * g), out_shape=jax.S...  69.1 us
    pallas_call x1, Pallas kernels, entry(): pl.pallas_call(entry_kernel, out_shape=(shape((rows, width), f32), shape(...  46.3 us
    pallas_call x1, Pallas kernels, attend_forward(): pl.pallas_call(forward_kernel, out_shape=(jax.ShapeDtypeStruct((n, width)...  37.4 us
    pallas_call x1, Pallas kernels, leave(): pl.pallas_call(exit_kernel, out_shape=(shape((rows, width), f32), shape((...  30.6 us
    ppermute x10, starting transfers between devices, turn(): return lax.ppermute(value, AXES, pairs)  15.5 us
    dot_general x2, matrix products, mm(): return lax.dot_general(a, b, dims, preferred_element_type=jnp.float32)  10.4 us
  transfers between devices with their start and end apart: 15, of which 1 were waited for; matrix products, arithmetic and copies ran while one was open for 3% of the time, Pallas kernels for 31%

commit v1 on v0

--- a/solution.py
+++ b/solution.py
@@ -262,11 +262,12 @@
     dp, tensor = lax.axis_index("dp"), lax.axis_index("tensor")
     inner = tensor % 2
     partner = (dp, tensor + 1 - 2 * inner)
-    z = dp // 2
+    z, x = dp // 2, dp % 2
+    to_x = (2 * z + 1 - x, tensor)
     to_y = (dp, (tensor + 2) % 4)
     mine = pl.multiple_of(inner * rows, 1024)
     theirs = pl.multiple_of((1 - inner) * rows, 1024)
-    greet([partner, to_y] if pieces else [partner])
+    greet([partner, to_x, to_y] if pieces else [partner])
 
     def remote(n, src, dst, device=partner):
         return pltpu.make_async_remote_copy(src, dst, send.at[n], recv.at[n], device_id=device,
@@ -309,11 +310,12 @@
         second = second + weight(downs, wd_ref)
     late = load(cot, c_ref)
     if pieces:
-        by_y = []
-        for k in range(4):
-            held[k].wait()
-            by_y.append(remote(12 + k, block(0, zs[k]), block(1, zs[k]), to_y))
-            by_y[k].start()
+        for copy in held:
+            copy.wait()
+        by_y = [remote(12 + m, block(0, 2 * x + m), block(1, 2 * x + m), to_y) for m in range(2)]
+        by_x = [remote(14 + m, block(1, 2 * x + m), block(1, 2 * x + m), to_x) for m in range(2)]
+        for copy in by_y:
+            copy.start()
     vec = lambda n: vec_ref[n:n + 1, :]
     sums_ref[...] = jnp.zeros_like(sums_ref)
     upsum_ref[...] = jnp.zeros_like(upsum_ref)
@@ -370,6 +372,9 @@
         inv_ref[r, :] = inv
         hl_ref[r, :] = bf(hat * vec(1) + vec(2))
     strips(first_norm)
+    if pieces:
+        by_y[0].wait_recv()
+        by_x[0].start()
     for b in range(blocks):
         hlt_ref[:, BLOCK * b:BLOCK * b + BLOCK] = hl_ref[BLOCK * b:BLOCK * b + BLOCK, :].T
     acc_ref[...] = jnp.zeros_like(acc_ref)
@@ -384,10 +389,17 @@
                 swaps[1 + 2 * o].wait()
                 swaps[2 + 2 * o].wait()
         if pieces:
+            @pl.when(j == 2)
+            def _():
+                by_y[1].wait_recv()
+                by_x[1].start()
+
             @pl.when(j == 1)
             def _():
+                for copy in by_x:
+                    copy.wait()
                 for copy in by_y:
-                    copy.wait()
+                    copy.wait_send()
                 swaps[4].start()
 
         def lift(b):
@@ -622,9 +634,9 @@
     pl.semaphore_wait(barrier, len(devices))
 
 
-def entry_kernel(tokens, pos_ref, mem_ref, wq_ref, bq_ref, bu_ref, wu_ref, wd_ref, wo_ref,
+def entry_kernel(tokens, pos_ref, mem_in, wq_in, bq_ref, bu_in, wu_ref, wd_ref, wo_ref,
                  x0_out, x_out, q_out, k_out, v_out, w_out, up_g, down_g, out_g, bu_out,
-                 x0_ref, x_ref, g_ref, b_ref, y_ref, third_ref, q_ref, k_ref, v_ref, ub_ref, send, recv, sem):
+                 x0_ref, x_ref, g_ref, b_ref, y_ref, third_ref, q_ref, k_ref, v_ref, ub_ref, wq_ref, bu_ref, mem_ref, send, recv, sem):
     f32, bf16 = jnp.float32, jnp.bfloat16
     rows, width = x0_ref.shape
     dp, tensor = lax.axis_index("dp"), lax.axis_index("tensor")
@@ -638,6 +650,17 @@
     to_y = (dp, (tensor + 2) % 4)
     to_core = (dp, tensor + 1 - 2 * inner)
     to_both = (dp, 3 - tensor)
+    heads = [wq_in[n, :, 0:128].astype(f32) for n in range(3)]
+    values = [wq_in[n, :, 128:192].astype(f32) for n in range(3)]
+    lane = lax.broadcasted_iota(jnp.int32, heads[0].shape, 1)
+    wq_ref[:, 0:128] = jnp.where(lane < 64, heads[0], pltpu.roll(heads[1], 64, 1)).astype(bf16)
+    wq_ref[:, 128:256] = jnp.where(lane < 64, pltpu.roll(heads[0], 64, 1), heads[1]).astype(bf16)
+    wq_ref[:, 256:384] = jnp.concatenate(values[0:2], axis=1).astype(bf16)
+    wq_ref[:, 384:512] = wq_in[2, :, 0:128]
+    wq_ref[:, 512:576] = wq_in[2, :, 128:192]
+    bu_ref[...] = jnp.broadcast_to(bu_in[...].astype(f32), bu_ref.shape).astype(bf16)
+    mem_ref[...] = jnp.zeros_like(mem_ref)
+    mem_ref[0:mem_in.shape[0], :] = mem_in[...]
     greet(to_z[1:] + [to_x, to_y, to_core, to_both])
     ex = Exchange(send, recv)
     started = []
@@ -758,7 +781,7 @@
         copy.wait()
 
 
-def entry(tokens, positions, memory_rows, shard_qkv, biases, up_bias, up, down, out):
+def entry(tokens, positions, memory_rows, qkv_heads, biases, up_bias, up, down, out):
     f32, bf16 = jnp.float32, jnp.bfloat16
     rows, width = tokens.shape
     r = up.shape[0]
@@ -775,13 +798,13 @@
         scratch_shapes=[
             v((rows, width), f32), v((2 * rows, width), bf16), v((2, 8, r, 576), bf16), v((2, 16, 640), bf16),
             v((BLOCK, 640), f32), v((2 * rows, 256), f32), v((2 * rows, 384), bf16), v((2 * rows, 384), bf16), v((2 * rows, 384), bf16),
-            v((3, 16, up.shape[1]), bf16),
+            v((3, 16, up.shape[1]), bf16), v((r, 576), bf16), v((16, up.shape[1]), bf16), v((32, width), bf16),
             pltpu.SemaphoreType.DMA((48,)), pltpu.SemaphoreType.DMA((48,)), pltpu.SemaphoreType.DMA((16,)),
         ],
         compiler_params=pltpu.CompilerParams(vmem_limit_bytes=VMEM_MAX, collective_id=0, has_side_effects=True),
         cost_estimate=pl.CostEstimate(flops=4 * rows * width * 1152, bytes_accessed=20_000_000, transcendentals=0),
         name="entry",
-    )(tokens, positions, memory_rows, shard_qkv, biases, up_bias, up, down, out)
+    )(tokens, positions, memory_rows, qkv_heads, biases, up_bias, up, down, out)
 
 
 def exit_kernel(x_all, d0, d1, d2, w_all, third, kept_ref, came_ref, dr1, pos_ref, sums_in, up_in,
@@ -1125,8 +1148,7 @@
     if fused:
         memory = memory_positions.shape[1]
         place = jnp.pad(positions[None], ((0, 7), (0, 32 - memory)), constant_values=-1)
-        table = jnp.pad(memory_rows, ((0, 32 - memory), (0, 0)))
-        x0, x_all, q, k, v, w_qkv, up_g, down_g, out_g, b_up = entry(tokens, place, table, shard_qkv, bias_qkv, own_up_bias, up_weight, down_weight, shard_out)
+        x0, x_all, q, k, v, w_qkv, up_g, down_g, out_g, b_up = entry(tokens, place, memory_rows, qkv_weight.transpose(1, 0, 2), bias_qkv, up_bias[None], up_weight, down_weight, shard_out)
         column = jnp.pad(jnp.broadcast_to(positions[:, None], (memory, 128)), ((0, 32 - memory), (0, 0)), constant_values=-1)
         w_qkv = w_qkv.reshape(2, width, 9 * hd)
         third = jnp.concatenate([w_qkv[o][:, (6 + n) * hd:(7 + n) * hd] for n in range(3) for o in range(2)], 1)
@@ -1298,23 +1320,40 @@
     )(jnp.stack([x, z]), kept_down, kept_up, kept_out, came_x, came_y, first.reshape(zs, 2, r, first.shape[-1]))
 
 
-def spread_kernel(t_ref, kept, came_one, came_two, came_three, small, down, up, out, memory, vec, up_bias, qv):
+def spread_kernel(t_ref, kept, came_one, came_two, came_three, small, one, two,
+                  down, up, out, memory, up_bias, qkv, qv, *vectors):
     f32 = jnp.float32
     width = down.shape[1]
-    for ref, start in ((down, 0), (up, width), (out, 2 * width)):
-        cols = slice(start, start + ref.shape[1])
-        ref[...] = (kept[:, cols] + came_one[:, cols].astype(f32)) + (came_two[:, cols].astype(f32) + came_three[:, cols].astype(f32))
+    total = lambda cols: ((kept[:, cols] + came_one[:, cols].astype(f32))
+                          + (came_two[:, cols].astype(f32) + came_three[:, cols].astype(f32)))
+    down[...] = total(slice(0, width))
+    up[...] = total(slice(width, 2 * width))
+    out[...] = total(slice(2 * width, 2 * width + 256)).T[0:192, :]
     half = width // 2
     t = t_ref[0]
     for h in range(2):
         cols = slice(half * h, half * h + half)
         memory[:, cols] = small[h, 0:memory.shape[0], :]
-        vec[:, cols] = small[h, 24:32, :]
-        up_bias[:, cols] = small[h, pl.ds(30 + t, 1), :]
         qv[h:h + 1, :] = small[h, pl.ds(34 + t, 1), :]
-
-
-def spread(tensor, kept, came, small, memory, ow):
+        for n, ref in enumerate(vectors):
+            ref[cols] = small[h, 24 + n, :]
+        up_bias[cols] = small[h, pl.ds(30 + t, 1), :].reshape(half)
+    turn = lambda value: pltpu.roll(value, 64, 1)
+    q, k, v = [one[:, 128 * n:128 * n + 128] for n in range(3)]
+    lane = lax.broadcasted_iota(jnp.int32, q.shape, 1)
+    qkv[0, :, 0:128] = jnp.where(lane < 64, q, turn(k))
+    qkv[0, :, 128:192] = v[:, 0:64]
+    qkv[1, :, 0:128] = jnp.where(lane < 64, turn(q), k)
+    qkv[1, :, 128:192] = turn(v)[:, 0:64]
+    n = two.shape[1]
+    lane = lax.broadcasted_iota(jnp.int32, two.shape[1:], 1)
+    qkv[2, 0:n, 0:128] = jnp.where(lane < 64, two[0], turn(two[1]))
+    qkv[2, n:2 * n, 0:128] = jnp.where(lane < 64, turn(two[0]), two[1])
+    qkv[2, 0:n, 128:192] = two[2][:, 0:64]
+    qkv[2, n:2 * n, 128:192] = turn(two[2])[:, 0:64]
+
+
+def spread(tensor, kept, came, small, one, two, memory):
     f32 = jnp.float32
     r, columns = kept.shape
     width = 2 * small.shape[2]
@@ -1322,14 +1361,14 @@
     vmem = pl.BlockSpec(memory_space=pltpu.VMEM)
     return pl.pallas_call(
         spread_kernel,
-        out_shape=(shape((r, width), f32), shape((r, width), f32), shape((r, ow), f32), shape((memory, width), f32),
-                   shape((8, width), f32), shape((1, width), f32), shape((2, width // 2), f32)),
-        in_specs=[pl.BlockSpec(memory_space=pltpu.SMEM)] + [vmem] * 5,
-        out_specs=[vmem] * 7,
+        out_shape=(shape((r, width), f32), shape((r, width), f32), shape((192, r), f32), shape((memory, width), f32),
+                   shape((width,), f32), shape((3, r, 192), f32), shape((2, width // 2), f32), *[shape((width,), f32)] * 6),
+        in_specs=[pl.BlockSpec(memory_space=pltpu.SMEM)] + [vmem] * 7,
+        out_specs=[vmem] * 13,
         compiler_params=pltpu.CompilerParams(vmem_limit_bytes=VMEM_MAX),
         cost_estimate=pl.CostEstimate(flops=3 * r * columns, bytes_accessed=3_000_000, transcendentals=0),
         name="spread",
-    )(tensor.reshape(1), kept, *came, small)
+    )(tensor.reshape(1), kept, *came, small, one, two)
 
 
 def finish_small(grid, tensor, x_all, q, k, v, do_all, mixed, lse, segments, w_qkv, third, dr1, column, sums, up_sums, block_out,
@@ -1358,16 +1397,13 @@
     over_z = [lambda a, n=n: grid.turn(a, 0, n) for n in range(1, 4)]
     came, d_two, q = beside(2, q, list(zip(sends, over_z + [over_x])))
     grad_tokens, one, two, small = leave(x_all, (d_zero, d_one, d_two), w_qkv, third, kept_first, came[3], dr1, column, sums, up_sums)
-    grad_down, grad_up, grad_out, grad_memory, vec, up_bias, qv = spread(tensor, kept, came[:3], small, 20, out.shape[-1])
+    grad_down, grad_up, grad_out, grad_memory, up_bias, grad_qkv, qv, *vec = spread(tensor, kept, came[:3], small, one, two, 20)
     hd = 64
-    slice_rows = one.shape[0]
-    two = two.reshape(3, slice_rows // 2, 2, hd).transpose(2, 1, 0, 3).reshape(slice_rows, 1, 3, hd)
-    grad_qkv = jnp.concatenate([one.reshape(slice_rows, 3, 2, hd).transpose(0, 2, 1, 3), two], 1).reshape(slice_rows, 3, 3 * hd)
     part = lambda n: jnp.concatenate([qv[0, 128 * n:128 * n + 128].reshape(2, hd), qv[1:2, 128 * n:128 * n + hd]])
     grad_qv = jnp.concatenate([part(0), part(2)], 1)
     t_out_bias, t_g1, t_s1, t_down_bias, t_g2, t_s2 = [vec[n] for n in (5, 3, 4, 2, 0, 1)]
-    return (block_out, grad_tokens, grad_memory, grad_qkv, grad_qv,
-            grad_out[:, :hw].reshape(slice_rows, 3, hd), t_out_bias, t_g1, t_s1, grad_up, up_bias.reshape(width), grad_down,
+    return (block_out, grad_tokens, grad_memory, grad_qkv.transpose(1, 0, 2), grad_qv,
+            grad_out.reshape(3, hd, -1).transpose(2, 0, 1), t_out_bias, t_g1, t_s1, grad_up, up_bias, grad_down,
             t_down_bias, t_g2, t_s2)
 
 

time: 349 us -> 338 us (0.968)
  local copies, waits for them, and re-layouts: 29.8 us -> 21.5 us
  starting transfers between devices: 21.2 us -> 17.6 us
    pallas_call x3, Pallas kernels: 69.1 us -> 75 us  [attend_backward(): pl.pallas_call(functools.partial(backward_kernel, 2 * g), out_shape=jax.S...]
    pallas_call x1, Pallas kernels: 84.2 us -> 78.5 us  [middle(): pl.pallas_call(kernel, out_shape=(shape((rows, width), bf16), shape((rows...]
    pallas_call x1, Pallas kernels: 37.4 us -> 41.1 us  [attend_forward(): pl.pallas_call(forward_kernel, out_shape=(jax.ShapeDtypeStruct((n, width)...]
  transfers between devices with their start and end apart: 15 -> 15, of which waited for: 1 -> 0; matrix products, arithmetic and copies ran while one was open for 3% -> 3% of each run, Pallas kernels for 31% -> 35%
where the time goes in v1:
time: 338 us; the launch traced here: 334 us
  Pallas kernels  281 us (83%)
  local copies, waits for them, and re-layouts  21.5 us (6%)
  starting transfers between devices  17.6 us (5%)
  matrix products  10.4 us (3%)
    pallas_call x1, Pallas kernels, middle(): pl.pallas_call(kernel, out_shape=(shape((rows, width), bf16), shape((rows...  78.5 us
    pallas_call x3, Pallas kernels, attend_backward(): pl.pallas_call(functools.partial(backward_kernel, 2 * g), out_shape=jax.S...  75 us
    pallas_call x1, Pallas kernels, entry(): pl.pallas_call(entry_kernel, out_shape=(shape((rows, width), f32), shape(...  46.4 us
    pallas_call x1, Pallas kernels, attend_forward(): pl.pallas_call(forward_kernel, out_shape=(jax.ShapeDtypeStruct((n, width)...  41.1 us
    pallas_call x1, Pallas kernels, leave(): pl.pallas_call(exit_kernel, out_shape=(shape((rows, width), f32), shape((...  28.2 us
    ppermute x10, starting transfers between devices, turn(): return lax.ppermute(value, AXES, pairs)  12.4 us
    dot_general x2, matrix products, mm(): return lax.dot_general(a, b, dims, preferred_element_type=jnp.float32)  10.4 us
  transfers between devices with their start and end apart: 15, of which 0 were waited for; matrix products, arithmetic and copies ran while one was open for 3% of the time, Pallas kernels for 35%

profile of v1, /device:TPU:0, one launch (start us, length us, event | category | flops | bytes accessed | tf_op | source)
XLA Modules:
  0.0 333.9 jit_solution(5882192996662006848)
XLA Ops:
  0.7 0.8 reshape.80
  1.5 0.7 constant_dynamic-slice_fusion
  2.2 0.6 pad.18.pos_ref
  2.9 0.1 concatenate.15
  3.0 0.6 pad.19.bq_ref
  3.7 1.3 broadcast_in_dim.11.bu_in
  4.9 0.9 copy.33
  5.8 0.6 pad.20.wo_ref
  6.4 46.4 %entry.1 = (f32[1024,768]{1,0:T(8,128)}, bf16[2048,768]{1,0:T(8,128)(2,1)}, bf16[2048,384]{1,0:T(8,128)(2,1)}, bf16[2048,384]{1,0:T(8,128)(2,1)}, bf16[2048,384]...) custom-call(bf16[1024,768]{1,0:T(8,128)(2,1)} %tokens.1, ...), custom_call_target="tpu_custom_call" | custom-call | flops 3623878656 | bytes 20000000 | tf_op jit(solution)/shard_map/entry/pallas_call | solution.py:791
  52.9 1.0 collective-permute-start.1
  53.9 0.6 collective-permute-start.2
  54.5 4.4 %collective-permute-start.3 = (bf16[192,768]{1,0:T(8,128)(2,1)}, bf16[192,768]{1,0:T(8,128)(2,1)}, u32[]{:S(2)}, u32[]{:S(2)}) collective-permute-start(bf16[192,768]{1,0:T(8,128)(2,1)} %bitcast.46), channel_id=1, source_target_pairs={{0,16},{1,17},{2,18},{3,19},{4,20},{5,21},{6,22},{7,23},{8,24},{9,... | collective-permute-start | bytes 884744 | tf_op jit(solution)/shard_map/ppermute | solution.py:1033
  58.9 0.5 collective-permute-start.4
  59.4 0.6 collective-permute-start
  60.0 0.6 slice.72.first_ref
  60.6 0.6 slice.73.last_ref
  61.2 1.3 broadcast_in_dim.12.kseg_ref
  62.6 0.6 broadcast_in_dim.13.qseg_ref
  63.2 41.1 %attend_forward.1 = (bf16[2048,384]{1,0:T(8,128)(2,1)}, f32[8,2048]{1,0:T(8,128)}) custom-call(s32[8]{0:T(128)} %slice.72.first_ref, s32[8]{0:T(128)} %slice.73.last_ref, bf16[2048,384]{1,0:T(8,128)(2,1)} %get-tuple-element.146.q_ref, bf16[2048,384]{1,0:T(8,128)(2,1)} %get-tuple-element.96.k_ref, bf16[2048,384]{1,0:T(8,128)(2,1)} %get-tuple-element.97.v_ref, ...), custom_call_target="tpu_custom_call" | custom-call | flops 6442450944 | bytes 6291456 | tf_op jit(solution)/shard_map/attend_forward/pallas_call | solution.py:106
  104.5 0.6 convert_element_type.13.refs_9_
  105.2 78.5 %middle.1 = (bf16[1024,768]{1,0:T(8,128)(2,1)}, f32[1024,768]{1,0:T(8,128)}, bf16[2048,384]{1,0:T(8,128)(2,1)}, bf16[768,768]{1,0:T(8,128)(2,1)}, bf16[384,768]{...) custom-call(bf16[2048,384]{1,0:T(8,128)(2,1)} %get-tuple-element.98., ...), custom_call_target="tpu_custom_call" | custom-call | flops 32614907904 | bytes 60000000 | tf_op jit(solution)/shard_map/middle/pallas_call | solution.py:596
  183.7 0.2 collective-permute-start.7
  183.9 3.0 fusion
  186.9 1.9 collective-permute-start.5
  188.8 0.2 collective-permute-start.6
  189.0 25.1 %attend_backward.3.d1 = bf16[2048,384]{1,0:T(8,128)(2,1)} custom-call(s32[8]{0:T(128)} %slice.72.first_ref, s32[8]{0:T(128)} %slice.73.last_ref, bf16[2048,384]{1,0:T(8,128)(2,1)} %get-tuple-element.146.q_ref, bf16[2048,384]{1,0:T(8,128)(2,1)} %get-tuple-element.115.do_ref, bf16[2048,384]{1,0:T(8,128)(2,1)} %get-tuple-element.98.o_all.o_ref, ...), custom_call_target="tpu_custom_call" | custom-call | flops 5368709120 | bytes 3670016 | tf_op jit(solution)/shard_map/attend_backward/pallas_call | solution.py:210
  214.1 5.0 %convolution_convert_fusion = bf16[768,384]{1,0:T(8,128)(2,1)} fusion(bf16[2048,768]{1,0:T(8,128)(2,1)} %get-tuple-element.105.x_all, bf16[2048,384]{1,0:T(8,128)(2,1)} %attend_backward.3.d1), kind=kOutput, calls=%fused_computation.1 | convolution fusion | flops 1208254464 | bytes 5308416 | tf_op jit(solution)/shard_map/dot_general | solution.py:19
  219.2 4.9 %blend_one.1 = (f32[4,96,768]{2,1,0:T(8,128)}, f32[4,96,768]{2,1,0:T(8,128)}, f32[4,96,256]{2,1,0:T(8,128)}, bf16[4,96,1024]{2,1,0:T(8,128)(2,1)}, bf16[4,96,768]{2,1,0:T(8,128)(2,1)}) custom-call(s32[1]{0:T(128)} %bitcast.7.x_ref, bf16[4,2,96,768]{3,2,1,0:T(8,128)(2,1)} %bitcast.35, bf16[2,2,96,768]{3,2,1,0:T(8,128)(2,1)} %bitcast.36, ...), custom_call_target="tpu_custom_call" | custom-call | flops 2359296 | bytes 10000000 | tf_op jit(solution)/shard_map/blend_one/pallas_call | solution.py:1271
  224.2 1.6 fusion.1
  225.7 1.2 concatenate.16.third
  226.9 2.0 collective-permute-start.10
  229.0 0.6 pad_add_fusion.at_ref
  229.5 24.8 %attend_backward.4.d0 = bf16[2048,384]{1,0:T(8,128)(2,1)} custom-call(s32[8]{0:T(128)} %slice.72.first_ref, s32[8]{0:T(128)} %slice.73.last_ref, bf16[2048,384]{1,0:T(8,128)(2,1)} %get-tuple-element.146.q_ref, bf16[2048,384]{1,0:T(8,128)(2,1)} %get-tuple-element.115.do_ref, bf16[2048,384]{1,0:T(8,128)(2,1)} %get-tuple-element.98.o_all.o_ref, ...), custom_call_target="tpu_custom_call" | custom-call | flops 5368709120 | bytes 3670016 | tf_op jit(solution)/shard_map/attend_backward/pallas_call | solution.py:210
  254.4 5.4 %convolution_add_fusion = f32[768,384]{1,0:T(8,128)} fusion(bf16[2048,768]{1,0:T(8,128)(2,1)} %get-tuple-element.105.x_all, bf16[2048,384]{1,0:T(8,128)(2,1)} %attend_backward.4.d0, bf16[768,384]{1,0:T(8,128)(2,1)} %collective-permute-done.10), kind=kOutput, calls=%fused_computation | convolution fusion | flops 1208549376 | bytes 6488064 | tf_op jit(solution)/shard_map/dot_general | solution.py:19
  259.7 4.3 %blend_two.1 = (f32[96,1792]{1,0:T(8,128)}, f32[4,96,384]{2,1,0:T(8,128)}, bf16[96,1792]{1,0:T(8,128)(2,1)}, bf16[96,1792]{1,0:T(8,128)(2,1)}, bf16[96,1792]{1,0:T(8,128)(2,1)}, /*index=5*/bf16[4,96,384]{2,1,0:T(8,128)(2,1)}) custom-call(s32[2]{0:T(128)} %pad_add_fusion.at_ref, f32[4,96,768]{2,1,0:T(8,128)} %get-tuple-element.131.kept_down, ...), custom_call_target="tpu_custom_call" | custom-call | flops 2752512 | bytes 10000000 | tf_op jit(solution)/shard_map/blend_two/pallas_call | solution.py:1311
  264.1 1.9 collective-permute-start.11
  266.0 2.4 collective-permute-start.13
  268.4 1.7 collective-permute-start.14
  270.1 25.1 %attend_backward.5.d2 = bf16[2048,384]{1,0:T(8,128)(2,1)} custom-call(s32[8]{0:T(128)} %slice.72.first_ref, s32[8]{0:T(128)} %slice.73.last_ref, bf16[2048,384]{1,0:T(8,128)(2,1)} %get-tuple-element.146.q_ref, bf16[2048,384]{1,0:T(8,128)(2,1)} %get-tuple-element.115.do_ref, bf16[2048,384]{1,0:T(8,128)(2,1)} %get-tuple-element.98.o_all.o_ref, ...), custom_call_target="tpu_custom_call" | custom-call | flops 5368709120 | bytes 3670016 | tf_op jit(solution)/shard_map/attend_backward/pallas_call | solution.py:210
  295.3 0.7 pad.22.pos_ref
  295.9 28.2 %leave.1 = (f32[1024,768]{1,0:T(8,128)}, f32[96,384]{1,0:T(8,128)}, f32[3,48,128]{2,1,0:T(8,128)}, f32[2,40,384]{2,1,0:T(8,128)}) custom-call(bf16[2048,768]{1,0:T(8,128)(2,1)} %get-tuple-element.105.x_all, bf16[2048,384]{1,0:T(8,128)(2,1)} %attend_backward.4.d0, bf16[2048,384]{1,0:T(8,128)(2,1)} %attend_backward.3.d1, bf16[2048,384]{1,0:T(8,128)(2,1)} %attend_backward.5.d2, ...), custom_call_target="tpu_custom_call" | custom-call | flops 4831838208 | bytes 20000000 | tf_op jit(solution)/shard_map/leave/pallas_call | solution.py:971
  324.2 2.7 spread.1
  326.9 0.7 fusion.3
  327.6 0.7 slice_reduce_fusion.3
  328.3 0.1 reshape_squeeze.19
  328.5 0.7 maximum_maximum_fusion
  329.2 2.8 copy.36
  332.0 1.7 copy.37
  (56 shorter events, 0.5 us)
Async XLA Ops:
  0.6 59.4 %copy-start = (s32[2,2048]{1,0:T(2,128)S(1)}, s32[2,2048]{1,0:T(2,128)}, u32[]{:S(2)}) copy-start(s32[2,2048]{1,0:T(2,128)} %param.18) | copy-start | bytes 49156
  52.9 52.3 %collective-permute-start.1 = (bf16[768,768]{1,0:T(8,128)(2,1)}, bf16[768,768]{1,0:T(8,128)(2,1)}, u32[]{:S(2)}, u32[]{:S(2)}) collective-permute-start(bf16[768,768]{1,0:T(8,128)(2,1)} %bitcast.43), channel_id=1, source_target_pairs={{0,2},{1,3},{2,0},{3,1},{4,6},{5,7},{6,4},{7,5},{8,10},{9,11},{10,... | collective-permute-start | bytes 3538952 | tf_op jit(solution)/shard_map/ppermute | solution.py:1041
  53.9 51.2 %collective-permute-start.2 = (bf16[192,768]{1,0:T(8,128)(2,1)}, bf16[192,768]{1,0:T(8,128)(2,1)}, u32[]{:S(2)}, u32[]{:S(2)}) collective-permute-start(bf16[192,768]{1,0:T(8,128)(2,1)} %bitcast.45), channel_id=1, source_target_pairs={{0,8},{1,9},{2,10},{3,11},{4,12},{5,13},{6,14},{7,15},{8,16},{9,17... | collective-permute-start | bytes 884744 | tf_op jit(solution)/shard_map/ppermute | solution.py:1033
  54.5 50.7 %collective-permute-start.3 = (bf16[192,768]{1,0:T(8,128)(2,1)}, bf16[192,768]{1,0:T(8,128)(2,1)}, u32[]{:S(2)}, u32[]{:S(2)}) collective-permute-start(bf16[192,768]{1,0:T(8,128)(2,1)} %bitcast.46), channel_id=1, source_target_pairs={{0,16},{1,17},{2,18},{3,19},{4,20},{5,21},{6,22},{7,23},{8,24},{9,... | collective-permute-start | bytes 884744 | tf_op jit(solution)/shard_map/ppermute | solution.py:1033
  58.9 46.3 %collective-permute-start.4 = (bf16[192,768]{1,0:T(8,128)(2,1)}, bf16[192,768]{1,0:T(8,128)(2,1)}, u32[]{:S(2)}, u32[]{:S(2)}) collective-permute-start(bf16[192,768]{1,0:T(8,128)(2,1)} %bitcast.47), channel_id=1, source_target_pairs={{0,24},{1,25},{2,26},{3,27},{4,28},{5,29},{6,30},{7,31},{8,0},{9,1... | collective-permute-start | bytes 884744 | tf_op jit(solution)/shard_map/ppermute | solution.py:1033
  59.4 45.8 %collective-permute-start = (bf16[2,4,96,256]{3,2,1,0:T(8,128)(2,1)}, bf16[2,4,96,256]{3,2,1,0:T(8,128)(2,1)}, u32[]{:S(2)}, u32[]{:S(2)}) collective-permute-start(bf16[2,4,96,256]{3,2,1,0:T(8,128)(2,1)} %get-tuple-element.100.refs_0_), channel_id=1, source_target_pairs={{0,4},{1,5},{2,6},{3,7},{4,0},{5,1},{6,2},{7,3},{8,12},{9,13},{10,... | collective-permute-start | bytes 1179656 | tf_op jit(solution)/shard_map/ppermute | solution.py:1033
  63.2 41.2 %copy-start.3 = (bf16[768]{0:T(1024)(128)(2,1)S(1)}, bf16[768]{0:T(1024)(128)(2,1)}, u32[]{:S(2)}) copy-start(bf16[768]{0:T(1024)(128)(2,1)} %param.24) | copy-start | bytes 4612
  63.2 41.2 %copy-start.4 = (bf16[768]{0:T(1024)(128)(2,1)S(1)}, bf16[768]{0:T(1024)(128)(2,1)}, u32[]{:S(2)}) copy-start(bf16[768]{0:T(1024)(128)(2,1)} %param.25) | copy-start | bytes 4612
  63.2 41.2 %copy-start.5 = (bf16[768]{0:T(1024)(128)(2,1)S(1)}, bf16[768]{0:T(1024)(128)(2,1)}, u32[]{:S(2)}) copy-start(bf16[768]{0:T(1024)(128)(2,1)} %param.26) | copy-start | bytes 4612
  63.2 41.2 %copy-start.6 = (bf16[768]{0:T(1024)(128)(2,1)S(1)}, bf16[768]{0:T(1024)(128)(2,1)}, u32[]{:S(2)}) copy-start(bf16[768]{0:T(1024)(128)(2,1)} %param.30) | copy-start | bytes 4612
  63.2 41.2 %copy-start.7 = (bf16[768]{0:T(1024)(128)(2,1)S(1)}, bf16[768]{0:T(1024)(128)(2,1)}, u32[]{:S(2)}) copy-start(bf16[768]{0:T(1024)(128)(2,1)} %param.31) | copy-start | bytes 4612
  63.2 41.2 %copy-start.8 = (bf16[768]{0:T(1024)(128)(2,1)S(1)}, bf16[768]{0:T(1024)(128)(2,1)}, u32[]{:S(2)}) copy-start(bf16[768]{0:T(1024)(128)(2,1)} %param.32) | copy-start | bytes 4612
  183.7 30.4 %collective-permute-start.7 = (bf16[2,4,96,768]{3,2,1,0:T(8,128)(2,1)}, bf16[2,4,96,768]{3,2,1,0:T(8,128)(2,1)}, u32[]{:S(2)}, u32[]{:S(2)}) collective-permute-start(bf16[2,4,96,768]{3,2,1,0:T(8,128)(2,1)} %get-tuple-element.113), channel_id=1, source_target_pairs={{0,4},{1,5},{2,6},{3,7},{4,0},{5,1},{6,2},{7,3},{8,12},{9,13},{10,... | collective-permute-start | bytes 3538952 | tf_op jit(solution)/shard_map/ppermute | solution.py:1033
  183.9 4.9 %copy-start.9 = (s32[2,20]{1,0:T(2,128)S(1)}, s32[2,20]{1,0:T(2,128)}, u32[]{:S(2)}) copy-start(s32[2,20]{1,0:T(2,128)} %param.19) | copy-start | bytes 484
  186.9 27.2 %collective-permute-start.5 = (bf16[384,768]{1,0:T(8,128)(2,1)}, bf16[384,768]{1,0:T(8,128)(2,1)}, u32[]{:S(2)}, u32[]{:S(2)}) collective-permute-start(bf16[384,768]{1,0:T(8,128)(2,1)} %get-tuple-element.111), channel_id=1, source_target_pairs={{0,2},{1,3},{2,0},{3,1},{4,6},{5,7},{6,4},{7,5},{8,10},{9,11},{10,... | collective-permute-start | bytes 1769480 | tf_op jit(solution)/shard_map/ppermute | solution.py:1041
  188.8 25.3 %collective-permute-start.6 = (bf16[768,256]{1,0:T(8,128)(2,1)}, bf16[768,256]{1,0:T(8,128)(2,1)}, u32[]{:S(2)}, u32[]{:S(2)}) collective-permute-start(bf16[768,256]{1,0:T(8,128)(2,1)} %get-tuple-element.112), channel_id=1, source_target_pairs={{0,2},{1,3},{2,0},{3,1},{4,6},{5,7},{6,4},{7,5},{8,10},{9,11},{10,... | collective-permute-start | bytes 1179656 | tf_op jit(solution)/shard_map/ppermute | solution.py:1041
  224.1 30.2 %collective-permute-start.8 = (bf16[4,96,1024]{2,1,0:T(8,128)(2,1)}, bf16[4,96,1024]{2,1,0:T(8,128)(2,1)}, u32[]{:S(2)}, u32[]{:S(2)}) collective-permute-start(bf16[4,96,1024]{2,1,0:T(8,128)(2,1)} %get-tuple-element.126), channel_id=1, source_target_pairs={{0,4},{1,5},{2,6},{3,7},{4,0},{5,1},{6,2},{7,3},{8,12},{9,13},{10,... | collective-permute-start | bytes 2359304 | tf_op jit(solution)/shard_map/ppermute | solution.py:1033
  226.9 27.4 %collective-permute-start.9 = (bf16[4,96,768]{2,1,0:T(8,128)(2,1)}, bf16[4,96,768]{2,1,0:T(8,128)(2,1)}, u32[]{:S(2)}, u32[]{:S(2)}) collective-permute-start(bf16[4,96,768]{2,1,0:T(8,128)(2,1)} %get-tuple-element.127), channel_id=1, source_target_pairs={{0,2},{1,3},{2,0},{3,1},{4,6},{5,7},{6,4},{7,5},{8,10},{9,11},{10,... | collective-permute-start | bytes 1769480 | tf_op jit(solution)/shard_map/ppermute | solution.py:1041
  226.9 27.4 %collective-permute-start.10 = (bf16[768,384]{1,0:T(8,128)(2,1)}, bf16[768,384]{1,0:T(8,128)(2,1)}, u32[]{:S(2)}, u32[]{:S(2)}) collective-permute-start(bf16[768,384]{1,0:T(8,128)(2,1)} %convolution_convert_fusion), channel_id=1, source_target_pairs={{0,2},{1,3},{2,0},{3,1},{4,6},{5,7},{6,4},{7,5},{8,10},{9,11},{10,... | collective-permute-start | bytes 1769480 | tf_op jit(solution)/shard_map/ppermute | solution.py:1041
  264.1 31.2 %collective-permute-start.11 = (bf16[96,1792]{1,0:T(8,128)(2,1)}, bf16[96,1792]{1,0:T(8,128)(2,1)}, u32[]{:S(2)}, u32[]{:S(2)}) collective-permute-start(bf16[96,1792]{1,0:T(8,128)(2,1)} %get-tuple-element.142), channel_id=1, source_target_pairs={{0,8},{1,9},{2,10},{3,11},{4,12},{5,13},{6,14},{7,15},{8,16},{9,17... | collective-permute-start | bytes 1032200 | tf_op jit(solution)/shard_map/ppermute | solution.py:1033
  266.0 29.2 %collective-permute-start.12 = (bf16[96,1792]{1,0:T(8,128)(2,1)}, bf16[96,1792]{1,0:T(8,128)(2,1)}, u32[]{:S(2)}, u32[]{:S(2)}) collective-permute-start(bf16[96,1792]{1,0:T(8,128)(2,1)} %get-tuple-element.143), channel_id=1, source_target_pairs={{0,16},{1,17},{2,18},{3,19},{4,20},{5,21},{6,22},{7,23},{8,24},{9,... | collective-permute-start | bytes 1032200 | tf_op jit(solution)/shard_map/ppermute | solution.py:1033
  266.0 29.2 %collective-permute-start.13 = (bf16[96,1792]{1,0:T(8,128)(2,1)}, bf16[96,1792]{1,0:T(8,128)(2,1)}, u32[]{:S(2)}, u32[]{:S(2)}) collective-permute-start(bf16[96,1792]{1,0:T(8,128)(2,1)} %get-tuple-element.144), channel_id=1, source_target_pairs={{0,24},{1,25},{2,26},{3,27},{4,28},{5,29},{6,30},{7,31},{8,0},{9,1... | collective-permute-start | bytes 1032200 | tf_op jit(solution)/shard_map/ppermute | solution.py:1033
  268.4 26.8 %collective-permute-start.14 = (bf16[4,96,384]{2,1,0:T(8,128)(2,1)}, bf16[4,96,384]{2,1,0:T(8,128)(2,1)}, u32[]{:S(2)}, u32[]{:S(2)}) collective-permute-start(bf16[4,96,384]{2,1,0:T(8,128)(2,1)} %get-tuple-element.145), channel_id=1, source_target_pairs={{0,4},{1,5},{2,6},{3,7},{4,0},{5,1},{6,2},{7,3},{8,12},{9,13},{10,... | collective-permute-start | bytes 884744 | tf_op jit(solution)/shard_map/ppermute | solution.py:1033
  329.2 2.8 copy-start.2
  332.0 1.7 copy-start.1

commit v2 on v1

--- a/solution.py
+++ b/solution.py
@@ -389,13 +389,11 @@
                 swaps[1 + 2 * o].wait()
                 swaps[2 + 2 * o].wait()
         if pieces:
-            @pl.when(j == 2)
-            def _():
+            def relay():
                 by_y[1].wait_recv()
                 by_x[1].start()
 
-            @pl.when(j == 1)
-            def _():
+            def arrive():
                 for copy in by_x:
                     copy.wait()
                 for copy in by_y:
@@ -408,12 +406,16 @@
         for b in range(blocks):
             if b + 1 < blocks:
                 lift(b + 1)
+            if pieces and b == blocks // 2:
+                pl.when(j == 2)(relay)
             r = slice(BLOCK * b, BLOCK * b + BLOCK)
             for i in range(0, BLOCK, 32):
                 for w in range(0, part, 256):
                     z, gp = normal_cdf_parts(bufs[b % 2][i:i + 32, w:w + 256])
                     z_ref[j, BLOCK * b + i:BLOCK * b + i + 32, w:w + 256] = bf(z)
                     gp_ref[j, BLOCK * b + i:BLOCK * b + i + 32, w:w + 256] = gp
+            if pieces and b == 0:
+                pl.when(j == 1)(arrive)
             acc_ref[r, :] = acc_ref[r, :] + mm(z_ref[j, r, :], wd_ref[j], NT)
         return carry
     lax.fori_loop(0, 4, forward, 0)
@@ -807,9 +809,9 @@
     )(tokens, positions, memory_rows, qkv_heads, biases, up_bias, up, down, out)
 
 
-def exit_kernel(x_all, d0, d1, d2, w_all, third, kept_ref, came_ref, dr1, pos_ref, sums_in, up_in,
+def exit_kernel(x_all, d0, d1, d2, w_all, kept_ref, came_ref, dr1, pos_ref, sums_in, up_in,
                 tok_out, first_out, second_out, small_out,
-                x_ref, xt_ref, d_ref, w_ref, dr_ref, g_ref, own_ref, oth_ref, yb_ref, xs_ref, xb_ref, zt_ref, zs_ref, zb_ref,
+                x_ref, xt_ref, d_ref, w_ref, third_ref, dr_ref, g_ref, own_ref, oth_ref, yb_ref, xs_ref, xb_ref, zt_ref, zs_ref, zb_ref,
                 fs_ref, fb_ref, their_ref, got_ref, tok_ref, s_ref, t_ref, r_ref, first_ref, send, recv, sem):
     f32, bf16 = jnp.float32, jnp.bfloat16
     rows, width = dr_ref.shape
@@ -825,8 +827,7 @@
     far_z = to_z[2]
     loads = []
     for src, dst in ((d2, d_ref.at[2]), (x_all, x_ref), (d0, d_ref.at[0]), (d1, d_ref.at[1]),
-                     (w_all.at[0, :, pl.ds(0, 384)], w_ref.at[0]), (w_all.at[1, :, pl.ds(0, 384)], w_ref.at[1]),
-                     (third, w_ref.at[2]), (dr1, dr_ref)):
+                     (w_all, w_ref), (dr1, dr_ref)):
         copy = pltpu.make_async_copy(src, dst, sem.at[len(loads)])
         copy.start()
         loads.append(copy)
@@ -872,8 +873,17 @@
     own_place = lax.broadcasted_iota(jnp.int32, (32, rows), 1) + inner * rows
     own_picks = jnp.where(own_place == pos_ref[:, 0:1], 1.0, 0.0)
     memory = lax.dot_general(own_picks, dr_ref[...], NN, precision=lax.Precision.HIGHEST, preferred_element_type=f32)
+    lane = lax.broadcasted_iota(jnp.int32, (BLOCK, 128), 1)
+    for m in range(0, width, BLOCK):
+        r = slice(m, m + BLOCK)
+        own, far = [w_ref[o, r, 384:512].astype(f32) for o in range(2)]
+        third_ref[r, 0:128] = jnp.where(lane < 64, own, pltpu.roll(far, 64, 1)).astype(bf16)
+        third_ref[r, 128:256] = jnp.where(lane < 64, pltpu.roll(own, 64, 1), far).astype(bf16)
+        last = [w_ref[o, r, 512:576].astype(f32) for o in range(2)]
+        third_ref[r, 256:384] = jnp.concatenate(last, axis=1).astype(bf16)
+    sides = lambda n: third_ref[...] if n == 2 else w_ref[n, :, 0:384]
     for n in range(3):
-        memory = memory + mm(picked[n].astype(bf16), w_ref[n], NT)
+        memory = memory + mm(picked[n].astype(bf16), sides(n), NT)
     hw = s_ref.shape[2]
 
     def put(row, value):
@@ -912,7 +922,7 @@
 
     def block(start):
         r = pl.ds(pl.multiple_of(start, BLOCK), BLOCK)
-        return mm(d_ref[0, r, :], w_ref[0], NT) + mm(d_ref[1, r, :], w_ref[1], NT) + mm(d_ref[2, r, :], w_ref[2], NT)
+        return mm(d_ref[0, r, :], sides(0), NT) + mm(d_ref[1, r, :], sides(1), NT) + mm(d_ref[2, r, :], sides(2), NT)
 
     def away(b, carry):
         their_ref[pl.ds(pl.multiple_of(b * BLOCK, BLOCK), BLOCK), :] = block(theirs + b * BLOCK).astype(bf16)
@@ -945,7 +955,7 @@
         tok_ref[r, :] = tok_ref[r, :] + got_ref[r, :].astype(f32) + dr_ref[r, :]
         return carry
     lax.fori_loop(0, rows // STRIP, finish, 0)
-    out = pltpu.make_async_copy(tok_ref, tok_out, sem.at[8])
+    out = pltpu.make_async_copy(tok_ref, tok_out, sem.at[6])
     out.start()
     hop(3)
     for copy in z_first:
@@ -962,7 +972,7 @@
     out.wait()
 
 
-def leave(x_all, d, w_qkv, third, first, came, dr1, place, sums, up_sums):
+def leave(x_all, d, w_qkv, first, came, dr1, place, sums, up_sums):
     f32, bf16 = jnp.float32, jnp.bfloat16
     rows, width = dr1.shape
     r, half = first.shape[1], first.shape[1] // 2
@@ -971,10 +981,10 @@
     return pl.pallas_call(
         exit_kernel,
         out_shape=(shape((rows, width), f32), shape((r, 384), f32), shape((3, half, 128), f32), shape((2, 40, width // 2), f32)),
-        in_specs=[hbm] * 6 + [vmem] * 2 + [hbm] + [vmem] * 3,
+        in_specs=[hbm] * 5 + [vmem] * 2 + [hbm] + [vmem] * 3,
         out_specs=[hbm] + [vmem] * 3,
         scratch_shapes=[
-            v((2 * rows, width), bf16), v((width, 2 * rows), bf16), v((3, 2 * rows, 384), bf16), v((3, width, 384), bf16),
+            v((2 * rows, width), bf16), v((width, 2 * rows), bf16), v((3, 2 * rows, 384), bf16), v((2, width, 576), bf16), v((width, 384), bf16),
             v((rows, width), f32), v((width, 384), f32), v((2, 4, 3, half, 128), f32), v((2, 4, 3, half, 128), bf16),
             v((2, 4, 3, half, 128), bf16), v((4, 3, half, 128), bf16), v((4, 3, half, 128), bf16), v((4, 3, half, 128), f32),
             v((3, 3, half, 128), bf16), v((3, 3, half, 128), bf16), v((3, r, 384), bf16), v((3, r, 384), bf16),
@@ -985,7 +995,7 @@
         compiler_params=pltpu.CompilerParams(vmem_limit_bytes=VMEM_MAX, collective_id=2, has_side_effects=True),
         cost_estimate=pl.CostEstimate(flops=2 * rows * width * 384 * 8, bytes_accessed=20_000_000, transcendentals=0),
         name="leave",
-    )(x_all, *d, w_qkv, third, first, came, dr1, place, sums, up_sums)
+    )(x_all, *d, w_qkv, first, came, dr1, place, sums, up_sums)
 
 
 def layer_norm(values, norm_gain, norm_shift):
@@ -1151,7 +1161,6 @@
         x0, x_all, q, k, v, w_qkv, up_g, down_g, out_g, b_up = entry(tokens, place, memory_rows, qkv_weight.transpose(1, 0, 2), bias_qkv, up_bias[None], up_weight, down_weight, shard_out)
         column = jnp.pad(jnp.broadcast_to(positions[:, None], (memory, 128)), ((0, 32 - memory), (0, 0)), constant_values=-1)
         w_qkv = w_qkv.reshape(2, width, 9 * hd)
-        third = jnp.concatenate([w_qkv[o][:, (6 + n) * hd:(7 + n) * hd] for n in range(3) for o in range(2)], 1)
         up_all = up_g.reshape(width, units)
         ups = (up_all, grid.swap(up_all, 2))
         down_pair = down_g.reshape(-1, units)
@@ -1177,7 +1186,7 @@
     (block_out, dr1, do_all, *grads, sums, up_sums) = middle(
         mixed, x0, outs, ups, downs, out_cotangent, vec, b_up)
     if fused:
-        return finish_small(grid, tensor, x_all, q, k, v, do_all, mixed, lse, segments, w_qkv, third, dr1, column, sums, up_sums, block_out,
+        return finish_small(grid, tensor, x_all, q, k, v, do_all, mixed, lse, segments, w_qkv, dr1, column, sums, up_sums, block_out,
                             grads, hw)
     g_down, g_up, g_out = grads
 
@@ -1371,7 +1380,7 @@
     )(tensor.reshape(1), kept, *came, small, one, two)
 
 
-def finish_small(grid, tensor, x_all, q, k, v, do_all, mixed, lse, segments, w_qkv, third, dr1, column, sums, up_sums, block_out,
+def finish_small(grid, tensor, x_all, q, k, v, do_all, mixed, lse, segments, w_qkv, dr1, column, sums, up_sums, block_out,
                  grads, hw):
     f32, bf16 = jnp.float32, jnp.bfloat16
     tie = lax.optimization_barrier
@@ -1396,7 +1405,7 @@
     kept, kept_first, *sends = blend_two(x, z, kept_down, kept_up, kept_out, came_x, came_y, first)
     over_z = [lambda a, n=n: grid.turn(a, 0, n) for n in range(1, 4)]
     came, d_two, q = beside(2, q, list(zip(sends, over_z + [over_x])))
-    grad_tokens, one, two, small = leave(x_all, (d_zero, d_one, d_two), w_qkv, third, kept_first, came[3], dr1, column, sums, up_sums)
+    grad_tokens, one, two, small = leave(x_all, (d_zero, d_one, d_two), w_qkv, kept_first, came[3], dr1, column, sums, up_sums)
     grad_down, grad_up, grad_out, grad_memory, up_bias, grad_qkv, qv, *vec = spread(tensor, kept, came[:3], small, one, two, 20)
     hd = 64
     part = lambda n: jnp.concatenate([qv[0, 128 * n:128 * n + 128].reshape(2, hd), qv[1:2, 128 * n:128 * n + hd]])

time: 338 us -> 337 us (level)
  local copies, waits for them, and re-layouts: 21.5 us -> 15.8 us
  Pallas kernels: 281 us -> 286 us
    slice x2 -> x0, local copies, waits for them, and re-layouts: 4.53 us -> none  [shards(): w_qkv[o][:, (6 + n) * hd:(7 + n) * hd]]
    pallas_call x1, Pallas kernels: 78.5 us -> 82 us  [middle(): pl.pallas_call(kernel, out_shape=(shape((rows, width), bf16), shape((rows...]
  transfers between devices with their start and end apart: 15 -> 15, of which waited for: 0 -> 1; matrix products, arithmetic and copies ran while one was open for 3% -> 1% of each run, Pallas kernels for 35% -> 35%
where the time goes in v2:
time: 337 us; the launch traced here: 333 us
  Pallas kernels  286 us (85%)
  starting transfers between devices  17.8 us (5%)
  local copies, waits for them, and re-layouts  15.8 us (5%)
  matrix products  10.3 us (3%)
    pallas_call x1, Pallas kernels, middle(): pl.pallas_call(kernel, out_shape=(shape((rows, width), bf16), shape((rows...  82 us
    pallas_call x3, Pallas kernels, attend_backward(): pl.pallas_call(functools.partial(backward_kernel, 2 * g), out_shape=jax.S...  75 us
    pallas_call x1, Pallas kernels, entry(): pl.pallas_call(entry_kernel, out_shape=(shape((rows, width), f32), shape(...  46.4 us
    pallas_call x1, Pallas kernels, attend_forward(): pl.pallas_call(forward_kernel, out_shape=(jax.ShapeDtypeStruct((n, width)...  41.1 us
    pallas_call x1, Pallas kernels, leave(): pl.pallas_call(exit_kernel, out_shape=(shape((rows, width), f32), shape((...  29.5 us
    ppermute x10, starting transfers between devices, turn(): return lax.ppermute(value, AXES, pairs)  12.6 us
    dot_general x2, matrix products, mm(): return lax.dot_general(a, b, dims, preferred_element_type=jnp.float32)  10.3 us
  transfers between devices with their start and end apart: 15, of which 1 were waited for; matrix products, arithmetic and copies ran while one was open for 1% of the time, Pallas kernels for 35%

profile of v2, /device:TPU:0, one launch (start us, length us, event | category | flops | bytes accessed | tf_op | source)
XLA Modules:
  0.0 333.3 jit_solution(7518417440287110962)
XLA Ops:
  0.7 0.8 reshape.76
  1.5 0.7 constant_dynamic-slice_fusion
  2.2 0.6 pad.18.pos_ref
  2.9 0.1 concatenate.12
  3.0 0.6 pad.19.bq_ref
  3.7 0.9 copy.33
  4.5 0.6 pad.20.wo_ref
  5.2 1.3 broadcast_in_dim.11.bu_in
  6.4 46.4 %entry.1 = (f32[1024,768]{1,0:T(8,128)}, bf16[2048,768]{1,0:T(8,128)(2,1)}, bf16[2048,384]{1,0:T(8,128)(2,1)}, bf16[2048,384]{1,0:T(8,128)(2,1)}, bf16[2048,384]...) custom-call(bf16[1024,768]{1,0:T(8,128)(2,1)} %tokens.1, ...), custom_call_target="tpu_custom_call" | custom-call | flops 3623878656 | bytes 20000000 | tf_op jit(solution)/shard_map/entry/pallas_call | solution.py:793
  52.9 1.0 collective-permute-start.1
  53.9 0.6 collective-permute-start.2
  54.5 4.4 %collective-permute-start.3 = (bf16[192,768]{1,0:T(8,128)(2,1)}, bf16[192,768]{1,0:T(8,128)(2,1)}, u32[]{:S(2)}, u32[]{:S(2)}) collective-permute-start(bf16[192,768]{1,0:T(8,128)(2,1)} %bitcast.41), channel_id=1, source_target_pairs={{0,16},{1,17},{2,18},{3,19},{4,20},{5,21},{6,22},{7,23},{8,24},{9,... | collective-permute-start | bytes 884744 | tf_op jit(solution)/shard_map/ppermute | solution.py:1043
  58.9 0.5 collective-permute-start.4
  59.4 0.6 collective-permute-start
  60.0 0.6 slice.42.first_ref
  60.6 0.6 slice.43.last_ref
  61.2 1.4 broadcast_in_dim.12.kseg_ref
  62.6 0.6 broadcast_in_dim.13.qseg_ref
  63.2 41.1 %attend_forward.1 = (bf16[2048,384]{1,0:T(8,128)(2,1)}, f32[8,2048]{1,0:T(8,128)}) custom-call(s32[8]{0:T(128)} %slice.42.first_ref, s32[8]{0:T(128)} %slice.43.last_ref, bf16[2048,384]{1,0:T(8,128)(2,1)} %get-tuple-element.146.q_ref, bf16[2048,384]{1,0:T(8,128)(2,1)} %get-tuple-element.96.k_ref, bf16[2048,384]{1,0:T(8,128)(2,1)} %get-tuple-element.97.v_ref, ...), custom_call_target="tpu_custom_call" | custom-call | flops 6442450944 | bytes 6291456 | tf_op jit(solution)/shard_map/attend_forward/pallas_call | solution.py:106
  104.5 0.6 convert_element_type.13.refs_9_
  105.2 82.0 %middle.1 = (bf16[1024,768]{1,0:T(8,128)(2,1)}, f32[1024,768]{1,0:T(8,128)}, bf16[2048,384]{1,0:T(8,128)(2,1)}, bf16[768,768]{1,0:T(8,128)(2,1)}, bf16[384,768]{...) custom-call(bf16[2048,384]{1,0:T(8,128)(2,1)} %get-tuple-element.98., ...), custom_call_target="tpu_custom_call" | custom-call | flops 32614907904 | bytes 60000000 | tf_op jit(solution)/shard_map/middle/pallas_call | solution.py:598
  187.2 0.6 collective-permute-start.7
  187.8 1.5 collective-permute-start.5
  189.3 0.5 collective-permute-start.6
  189.8 25.1 %attend_backward.3.d1 = bf16[2048,384]{1,0:T(8,128)(2,1)} custom-call(s32[8]{0:T(128)} %slice.42.first_ref, s32[8]{0:T(128)} %slice.43.last_ref, bf16[2048,384]{1,0:T(8,128)(2,1)} %get-tuple-element.146.q_ref, bf16[2048,384]{1,0:T(8,128)(2,1)} %get-tuple-element.115.do_ref, bf16[2048,384]{1,0:T(8,128)(2,1)} %get-tuple-element.98.o_all.o_ref, ...), custom_call_target="tpu_custom_call" | custom-call | flops 5368709120 | bytes 3670016 | tf_op jit(solution)/shard_map/attend_backward/pallas_call | solution.py:210
  214.9 0.3 collective-permute-done.7.up_in
  215.2 5.0 %convolution_convert_fusion = bf16[768,384]{1,0:T(8,128)(2,1)} fusion(bf16[2048,768]{1,0:T(8,128)(2,1)} %get-tuple-element.105.x_all, bf16[2048,384]{1,0:T(8,128)(2,1)} %attend_backward.3.d1), kind=kOutput, calls=%fused_computation.1 | convolution fusion | flops 1208254464 | bytes 5308416 | tf_op jit(solution)/shard_map/dot_general | solution.py:19
  220.2 4.9 %blend_one.1 = (f32[4,96,768]{2,1,0:T(8,128)}, f32[4,96,768]{2,1,0:T(8,128)}, f32[4,96,256]{2,1,0:T(8,128)}, bf16[4,96,1024]{2,1,0:T(8,128)(2,1)}, bf16[4,96,768]{2,1,0:T(8,128)(2,1)}) custom-call(s32[1]{0:T(128)} %bitcast.7.x_ref, bf16[4,2,96,768]{3,2,1,0:T(8,128)(2,1)} %bitcast.30, bf16[2,2,96,768]{3,2,1,0:T(8,128)(2,1)} %bitcast.31, ...), custom_call_target="tpu_custom_call" | custom-call | flops 2359296 | bytes 10000000 | tf_op jit(solution)/shard_map/blend_one/pallas_call | solution.py:1280
  225.2 0.3 collective-permute-start.8
  225.5 1.8 collective-permute-start.10
  227.3 0.3 collective-permute-start.9
  227.6 0.6 pad_add_fusion.at_ref
  228.2 24.8 %attend_backward.4.d0 = bf16[2048,384]{1,0:T(8,128)(2,1)} custom-call(s32[8]{0:T(128)} %slice.42.first_ref, s32[8]{0:T(128)} %slice.43.last_ref, bf16[2048,384]{1,0:T(8,128)(2,1)} %get-tuple-element.146.q_ref, bf16[2048,384]{1,0:T(8,128)(2,1)} %get-tuple-element.115.do_ref, bf16[2048,384]{1,0:T(8,128)(2,1)} %get-tuple-element.98.o_all.o_ref, ...), custom_call_target="tpu_custom_call" | custom-call | flops 5368709120 | bytes 3670016 | tf_op jit(solution)/shard_map/attend_backward/pallas_call | solution.py:210
  253.0 5.3 %convolution_add_fusion = f32[768,384]{1,0:T(8,128)} fusion(bf16[2048,768]{1,0:T(8,128)(2,1)} %get-tuple-element.105.x_all, bf16[2048,384]{1,0:T(8,128)(2,1)} %attend_backward.4.d0, bf16[768,384]{1,0:T(8,128)(2,1)} %collective-permute-done.10), kind=kOutput, calls=%fused_computation | convolution fusion | flops 1208549376 | bytes 6488064 | tf_op jit(solution)/shard_map/dot_general | solution.py:19
  258.4 4.3 %blend_two.1 = (f32[96,1792]{1,0:T(8,128)}, f32[4,96,384]{2,1,0:T(8,128)}, bf16[96,1792]{1,0:T(8,128)(2,1)}, bf16[96,1792]{1,0:T(8,128)(2,1)}, bf16[96,1792]{1,0:T(8,128)(2,1)}, /*index=5*/bf16[4,96,384]{2,1,0:T(8,128)(2,1)}) custom-call(s32[2]{0:T(128)} %pad_add_fusion.at_ref, f32[4,96,768]{2,1,0:T(8,128)} %get-tuple-element.131.kept_down, ...), custom_call_target="tpu_custom_call" | custom-call | flops 2752512 | bytes 10000000 | tf_op jit(solution)/shard_map/blend_two/pallas_call | solution.py:1320
  262.6 1.8 collective-permute-start.11
  264.5 1.3 collective-permute-start.12
  265.8 1.2 collective-permute-start.13
  266.9 1.3 collective-permute-start.14
  268.2 25.1 %attend_backward.5.d2 = bf16[2048,384]{1,0:T(8,128)(2,1)} custom-call(s32[8]{0:T(128)} %slice.42.first_ref, s32[8]{0:T(128)} %slice.43.last_ref, bf16[2048,384]{1,0:T(8,128)(2,1)} %get-tuple-element.146.q_ref, bf16[2048,384]{1,0:T(8,128)(2,1)} %get-tuple-element.115.do_ref, bf16[2048,384]{1,0:T(8,128)(2,1)} %get-tuple-element.98.o_all.o_ref, ...), custom_call_target="tpu_custom_call" | custom-call | flops 5368709120 | bytes 3670016 | tf_op jit(solution)/shard_map/attend_backward/pallas_call | solution.py:210
  293.4 0.7 pad.22.pos_ref
  294.0 29.5 %leave.1 = (f32[1024,768]{1,0:T(8,128)}, f32[96,384]{1,0:T(8,128)}, f32[3,48,128]{2,1,0:T(8,128)}, f32[2,40,384]{2,1,0:T(8,128)}) custom-call(bf16[2048,768]{1,0:T(8,128)(2,1)} %get-tuple-element.105.x_all, bf16[2048,384]{1,0:T(8,128)(2,1)} %attend_backward.4.d0, bf16[2048,384]{1,0:T(8,128)(2,1)} %attend_backward.3.d1, bf16[2048,384]{1,0:T(8,128)(2,1)} %attend_backward.5.d2, ...), custom_call_target="tpu_custom_call" | custom-call | flops 4831838208 | bytes 20000000 | tf_op jit(solution)/shard_map/leave/pallas_call | solution.py:981
  323.5 2.7 spread.1
  326.3 0.7 slice_reduce_fusion.3
  327.0 0.7 fusion
  327.9 0.7 maximum_maximum_fusion
  328.5 2.8 copy.36
  331.3 1.7 copy.37
  (51 shorter events, 0.6 us)
Async XLA Ops:
  0.6 59.4 %copy-start = (s32[2,2048]{1,0:T(2,128)S(1)}, s32[2,2048]{1,0:T(2,128)}, u32[]{:S(2)}) copy-start(s32[2,2048]{1,0:T(2,128)} %param.18) | copy-start | bytes 49156
  52.9 52.3 %collective-permute-start.1 = (bf16[768,768]{1,0:T(8,128)(2,1)}, bf16[768,768]{1,0:T(8,128)(2,1)}, u32[]{:S(2)}, u32[]{:S(2)}) collective-permute-start(bf16[768,768]{1,0:T(8,128)(2,1)} %bitcast.38), channel_id=1, source_target_pairs={{0,2},{1,3},{2,0},{3,1},{4,6},{5,7},{6,4},{7,5},{8,10},{9,11},{10,... | collective-permute-start | bytes 3538952 | tf_op jit(solution)/shard_map/ppermute | solution.py:1051
  53.9 51.3 %collective-permute-start.2 = (bf16[192,768]{1,0:T(8,128)(2,1)}, bf16[192,768]{1,0:T(8,128)(2,1)}, u32[]{:S(2)}, u32[]{:S(2)}) collective-permute-start(bf16[192,768]{1,0:T(8,128)(2,1)} %bitcast.40), channel_id=1, source_target_pairs={{0,8},{1,9},{2,10},{3,11},{4,12},{5,13},{6,14},{7,15},{8,16},{9,17... | collective-permute-start | bytes 884744 | tf_op jit(solution)/shard_map/ppermute | solution.py:1043
  54.5 50.7 %collective-permute-start.3 = (bf16[192,768]{1,0:T(8,128)(2,1)}, bf16[192,768]{1,0:T(8,128)(2,1)}, u32[]{:S(2)}, u32[]{:S(2)}) collective-permute-start(bf16[192,768]{1,0:T(8,128)(2,1)} %bitcast.41), channel_id=1, source_target_pairs={{0,16},{1,17},{2,18},{3,19},{4,20},{5,21},{6,22},{7,23},{8,24},{9,... | collective-permute-start | bytes 884744 | tf_op jit(solution)/shard_map/ppermute | solution.py:1043
  58.9 46.3 %collective-permute-start.4 = (bf16[192,768]{1,0:T(8,128)(2,1)}, bf16[192,768]{1,0:T(8,128)(2,1)}, u32[]{:S(2)}, u32[]{:S(2)}) collective-permute-start(bf16[192,768]{1,0:T(8,128)(2,1)} %bitcast.42), channel_id=1, source_target_pairs={{0,24},{1,25},{2,26},{3,27},{4,28},{5,29},{6,30},{7,31},{8,0},{9,1... | collective-permute-start | bytes 884744 | tf_op jit(solution)/shard_map/ppermute | solution.py:1043
  59.4 45.8 %collective-permute-start = (bf16[2,4,96,256]{3,2,1,0:T(8,128)(2,1)}, bf16[2,4,96,256]{3,2,1,0:T(8,128)(2,1)}, u32[]{:S(2)}, u32[]{:S(2)}) collective-permute-start(bf16[2,4,96,256]{3,2,1,0:T(8,128)(2,1)} %get-tuple-element.100.refs_0_), channel_id=1, source_target_pairs={{0,4},{1,5},{2,6},{3,7},{4,0},{5,1},{6,2},{7,3},{8,12},{9,13},{10,... | collective-permute-start | bytes 1179656 | tf_op jit(solution)/shard_map/ppermute | solution.py:1043
  63.2 41.2 %copy-start.2 = (bf16[768]{0:T(1024)(128)(2,1)S(1)}, bf16[768]{0:T(1024)(128)(2,1)}, u32[]{:S(2)}) copy-start(bf16[768]{0:T(1024)(128)(2,1)} %param.24) | copy-start | bytes 4612
  63.2 41.2 %copy-start.3 = (bf16[768]{0:T(1024)(128)(2,1)S(1)}, bf16[768]{0:T(1024)(128)(2,1)}, u32[]{:S(2)}) copy-start(bf16[768]{0:T(1024)(128)(2,1)} %param.25) | copy-start | bytes 4612
  63.2 41.2 %copy-start.4 = (bf16[768]{0:T(1024)(128)(2,1)S(1)}, bf16[768]{0:T(1024)(128)(2,1)}, u32[]{:S(2)}) copy-start(bf16[768]{0:T(1024)(128)(2,1)} %param.26) | copy-start | bytes 4612
  63.2 41.2 %copy-start.5 = (bf16[768]{0:T(1024)(128)(2,1)S(1)}, bf16[768]{0:T(1024)(128)(2,1)}, u32[]{:S(2)}) copy-start(bf16[768]{0:T(1024)(128)(2,1)} %param.30) | copy-start | bytes 4612
  63.2 41.2 %copy-start.6 = (bf16[768]{0:T(1024)(128)(2,1)S(1)}, bf16[768]{0:T(1024)(128)(2,1)}, u32[]{:S(2)}) copy-start(bf16[768]{0:T(1024)(128)(2,1)} %param.31) | copy-start | bytes 4612
  63.2 41.2 %copy-start.7 = (bf16[768]{0:T(1024)(128)(2,1)S(1)}, bf16[768]{0:T(1024)(128)(2,1)}, u32[]{:S(2)}) copy-start(bf16[768]{0:T(1024)(128)(2,1)} %param.32) | copy-start | bytes 4612
  187.2 28.0 %collective-permute-start.7 = (bf16[2,4,96,768]{3,2,1,0:T(8,128)(2,1)}, bf16[2,4,96,768]{3,2,1,0:T(8,128)(2,1)}, u32[]{:S(2)}, u32[]{:S(2)}) collective-permute-start(bf16[2,4,96,768]{3,2,1,0:T(8,128)(2,1)} %get-tuple-element.113), channel_id=1, source_target_pairs={{0,4},{1,5},{2,6},{3,7},{4,0},{5,1},{6,2},{7,3},{8,12},{9,13},{10,... | collective-permute-start | bytes 3538952 | tf_op jit(solution)/shard_map/ppermute | solution.py:1043
  187.8 27.1 %collective-permute-start.5 = (bf16[384,768]{1,0:T(8,128)(2,1)}, bf16[384,768]{1,0:T(8,128)(2,1)}, u32[]{:S(2)}, u32[]{:S(2)}) collective-permute-start(bf16[384,768]{1,0:T(8,128)(2,1)} %get-tuple-element.111), channel_id=1, source_target_pairs={{0,2},{1,3},{2,0},{3,1},{4,6},{5,7},{6,4},{7,5},{8,10},{9,11},{10,... | collective-permute-start | bytes 1769480 | tf_op jit(solution)/shard_map/ppermute | solution.py:1051
  189.3 25.6 %collective-permute-start.6 = (bf16[768,256]{1,0:T(8,128)(2,1)}, bf16[768,256]{1,0:T(8,128)(2,1)}, u32[]{:S(2)}, u32[]{:S(2)}) collective-permute-start(bf16[768,256]{1,0:T(8,128)(2,1)} %get-tuple-element.112), channel_id=1, source_target_pairs={{0,2},{1,3},{2,0},{3,1},{4,6},{5,7},{6,4},{7,5},{8,10},{9,11},{10,... | collective-permute-start | bytes 1179656 | tf_op jit(solution)/shard_map/ppermute | solution.py:1051
  220.2 5.3 %copy-start.8 = (s32[2,20]{1,0:T(2,128)S(1)}, s32[2,20]{1,0:T(2,128)}, u32[]{:S(2)}) copy-start(s32[2,20]{1,0:T(2,128)} %param.19) | copy-start | bytes 484
  225.2 27.8 %collective-permute-start.8 = (bf16[4,96,1024]{2,1,0:T(8,128)(2,1)}, bf16[4,96,1024]{2,1,0:T(8,128)(2,1)}, u32[]{:S(2)}, u32[]{:S(2)}) collective-permute-start(bf16[4,96,1024]{2,1,0:T(8,128)(2,1)} %get-tuple-element.126), channel_id=1, source_target_pairs={{0,4},{1,5},{2,6},{3,7},{4,0},{5,1},{6,2},{7,3},{8,12},{9,13},{10,... | collective-permute-start | bytes 2359304 | tf_op jit(solution)/shard_map/ppermute | solution.py:1043
  225.5 27.5 %collective-permute-start.10 = (bf16[768,384]{1,0:T(8,128)(2,1)}, bf16[768,384]{1,0:T(8,128)(2,1)}, u32[]{:S(2)}, u32[]{:S(2)}) collective-permute-start(bf16[768,384]{1,0:T(8,128)(2,1)} %convolution_convert_fusion), channel_id=1, source_target_pairs={{0,2},{1,3},{2,0},{3,1},{4,6},{5,7},{6,4},{7,5},{8,10},{9,11},{10,... | collective-permute-start | bytes 1769480 | tf_op jit(solution)/shard_map/ppermute | solution.py:1051
  227.3 25.7 %collective-permute-start.9 = (bf16[4,96,768]{2,1,0:T(8,128)(2,1)}, bf16[4,96,768]{2,1,0:T(8,128)(2,1)}, u32[]{:S(2)}, u32[]{:S(2)}) collective-permute-start(bf16[4,96,768]{2,1,0:T(8,128)(2,1)} %get-tuple-element.127), channel_id=1, source_target_pairs={{0,2},{1,3},{2,0},{3,1},{4,6},{5,7},{6,4},{7,5},{8,10},{9,11},{10,... | collective-permute-start | bytes 1769480 | tf_op jit(solution)/shard_map/ppermute | solution.py:1051
  262.6 30.7 %collective-permute-start.11 = (bf16[96,1792]{1,0:T(8,128)(2,1)}, bf16[96,1792]{1,0:T(8,128)(2,1)}, u32[]{:S(2)}, u32[]{:S(2)}) collective-permute-start(bf16[96,1792]{1,0:T(8,128)(2,1)} %get-tuple-element.142), channel_id=1, source_target_pairs={{0,8},{1,9},{2,10},{3,11},{4,12},{5,13},{6,14},{7,15},{8,16},{9,17... | collective-permute-start | bytes 1032200 | tf_op jit(solution)/shard_map/ppermute | solution.py:1043
  264.5 28.9 %collective-permute-start.12 = (bf16[96,1792]{1,0:T(8,128)(2,1)}, bf16[96,1792]{1,0:T(8,128)(2,1)}, u32[]{:S(2)}, u32[]{:S(2)}) collective-permute-start(bf16[96,1792]{1,0:T(8,128)(2,1)} %get-tuple-element.143), channel_id=1, source_target_pairs={{0,16},{1,17},{2,18},{3,19},{4,20},{5,21},{6,22},{7,23},{8,24},{9,... | collective-permute-start | bytes 1032200 | tf_op jit(solution)/shard_map/ppermute | solution.py:1043
  265.8 27.6 %collective-permute-start.13 = (bf16[96,1792]{1,0:T(8,128)(2,1)}, bf16[96,1792]{1,0:T(8,128)(2,1)}, u32[]{:S(2)}, u32[]{:S(2)}) collective-permute-start(bf16[96,1792]{1,0:T(8,128)(2,1)} %get-tuple-element.144), channel_id=1, source_target_pairs={{0,24},{1,25},{2,26},{3,27},{4,28},{5,29},{6,30},{7,31},{8,0},{9,1... | collective-permute-start | bytes 1032200 | tf_op jit(solution)/shard_map/ppermute | solution.py:1043
  266.9 26.4 %collective-permute-start.14 = (bf16[4,96,384]{2,1,0:T(8,128)(2,1)}, bf16[4,96,384]{2,1,0:T(8,128)(2,1)}, u32[]{:S(2)}, u32[]{:S(2)}) collective-permute-start(bf16[4,96,384]{2,1,0:T(8,128)(2,1)} %get-tuple-element.145), channel_id=1, source_target_pairs={{0,4},{1,5},{2,6},{3,7},{4,0},{5,1},{6,2},{7,3},{8,12},{9,13},{10,... | collective-permute-start | bytes 884744 | tf_op jit(solution)/shard_map/ppermute | solution.py:1043
  328.5 2.8 copy-start.1
